TPU v7x, 128 devices: a whole 4x4x4 slice. The times are simulated.
128 devices in a mesh: row: 16 (over x_hi, y, core), rep: 8 (over x_lo, z).
Axes of the slice: x: 4 (x_hi: 2, x_lo: 2; x = x_hi * 2 + x_lo), y: 4, z: 4, core: 2. Of those that a mesh axis runs over, the one named last changes fastest.
Arguments:
- features: bfloat16 [65536, 1024], P('row', 'rep'), may hold values from -6 to 6
- tiles: bfloat16 [512, 16, 128, 128], P('row'), may hold values from -0.1875 to 0.1875
- columns: int32 [512, 16], P('row'), may hold values from 0 to 511
- counts: int32 [512], P('row'), may hold values from 1 to 16, as said below
- weight: bfloat16 [1024, 1024], P(None, 'rep'), may hold values from -0.1875 to 0.1875
- cotangent: bfloat16 [65536, 1024], P('row', 'rep'), may hold values from -6 to 6
Outputs:
- activations: bfloat16 [65536, 1024], P('row', 'rep')
- feature_grad: bfloat16 [65536, 1024], P('row', 'rep')
- weight_grad: float32 [1024, 1024], P('rep', 'row')
Inputs may be any that keep to these rules, and one draw needn't show every extreme that they name: `counts`: in every draw some row block has all 16 slots in use.
All inputs are finite; a program needn't handle non-finite values.
Results may differ from a plain program's by a relative error of at most 0.014.
Values may be sent and summed in bfloat16 or wider, within the bound.
A program may use at most 192 MiB of HBM per device.

v0:
```python
import jax
import jax.numpy as jnp
from jax import lax
from jax.sharding import PartitionSpec as P


def local(features, tiles, columns, counts, weight, cotangent):
    rows_here, feat_local = features.shape
    blocks_here, slots = columns.shape
    tile_size = tiles.shape[2]
    total_blocks = blocks_here * lax.axis_size("row")
    gathered = lax.all_gather(features, "row", axis=0, tiled=True)
    source_blocks = gathered.reshape(total_blocks, tile_size, feat_local)
    alive_mask = jnp.arange(slots)[None, :] < counts[:, None]
    masked_tiles = jnp.where(alive_mask[:, :, None, None], tiles, jnp.zeros((), tiles.dtype))
    operand = jnp.take(source_blocks, columns, axis=0)
    summed = jnp.einsum("bkij,bkjf->bif", masked_tiles, operand, preferred_element_type=jnp.float32)
    mixed = summed.reshape(rows_here, feat_local).astype(jnp.bfloat16)
    preact = jnp.dot(
        lax.all_gather(mixed, "rep", axis=1, tiled=True), weight, preferred_element_type=jnp.float32
    )
    sigmoid_pre = jax.nn.sigmoid(preact)
    activations = (preact * sigmoid_pre).astype(jnp.bfloat16)
    grad_out = (
        cotangent.astype(jnp.float32) * sigmoid_pre * (1.0 + preact * (1.0 - sigmoid_pre))
    ).astype(jnp.bfloat16)
    grad_cols = lax.all_gather(grad_out, "rep", axis=1, tiled=True)
    weight_terms = jnp.einsum("nf,nh->fh", mixed, grad_cols, preferred_element_type=jnp.float32)
    weight_grad = lax.psum_scatter(
        weight_terms.astype(jnp.bfloat16), "row", scatter_dimension=1, tiled=True
    ).astype(jnp.float32)
    full_weight = lax.all_gather(weight, "rep", axis=1, tiled=True)
    row_offset = lax.axis_index("rep") * feat_local
    own_rows = lax.dynamic_slice_in_dim(full_weight, row_offset, feat_local, 0)
    mixed_grad = jnp.einsum(
        "nh,fh->nf", grad_cols, own_rows, preferred_element_type=jnp.float32
    ).astype(jnp.bfloat16)
    grad_blocks = mixed_grad.reshape(blocks_here, tile_size, feat_local)
    contrib = jnp.einsum(
        "bkij,bif->bkjf", masked_tiles, grad_blocks, preferred_element_type=jnp.float32
    )
    scattered = jax.ops.segment_sum(
        contrib.reshape(blocks_here * slots, tile_size, feat_local),
        columns.reshape(-1),
        num_segments=total_blocks,
    )
    scattered = scattered.reshape(total_blocks * tile_size, feat_local)
    feature_grad = lax.psum_scatter(
        scattered.astype(jnp.bfloat16), "row", scatter_dimension=0, tiled=True
    )
    return (activations, feature_grad, weight_grad)


def solution(mesh):
    in_specs = (
        P("row", "rep"),
        P("row", None, None, None),
        P("row", None),
        P("row"),
        P(None, "rep"),
        P("row", "rep"),
    )
    out_specs = (P("row", "rep"), P("row", "rep"), P("rep", "row"))
    return jax.shard_map(local, mesh=mesh, in_specs=in_specs, out_specs=out_specs, check_vma=False)
```

profile of v0, /device:TPU:1, one launch (start us, length us, event | category | flops | bytes accessed | tf_op | source)
XLA Modules:
  0.0 712.6 jit_solution(94482328865075203)
XLA Ops:
  7.2 0.0 all-gather.5.cloned.1.call-start
  7.2 0.7 all-gather.5.cloned.1.call-update
  7.9 0.0 all-gather.7.cloned.1.call-start
  7.9 0.7 compare_and_fusion
  8.7 0.1 copy.11
  8.7 0.7 compare_select_fusion
  9.4 0.1 copy.12
  9.5 0.1 reshape.50
  9.6 0.7 iota_compare_fusion
  10.3 112.3 %all-gather.5.cloned.1.call-done = bf16[65536,128]{1,0:T(8,128)(2,1)} async-done(((bf16[4096,128]{1,0:T(8,128)(2,1)}), bf16[65536,128]{1,0:T(8,128)(2,1)}) %all-gather.5.cloned.1.call-update) | async-done | bytes 16777232 | tf_op jit(solution)/shard_map/all_gather | solution.py:12
  122.7 19.6 %gather_fusion = bf16[512,128,128]{2,1,0:T(8,128)(2,1)} fusion(bf16[512,128,128]{2,1,0:T(8,128)(2,1)} %bitcast.21, s32[1024]{0:T(1024)S(1)} %pad_clamp_fusion), kind=kCustom, calls=%fused_computation | custom fusion | bytes 33556480 | tf_op jit(solution)/shard_map/jit(_take)/gather | solution.py:16
  142.3 0.0 copy-start.1
  142.3 0.0 copy-start.3
  142.3 14.1 %bitcast_convert_fusion = bf16[32,128,128]{2,1,0:T(8,128)(2,1)} fusion(bf16[32,16,128,128]{3,2,1,0:T(8,128)(2,1)} %bitcast.22, pred[32,16]{1,0:T(8,128)(4,1)S(1)} %copy.11, bf16[32,16,128,128]{3,2,1,0:T(8,128)(2,1)} %param.7, pred[32,16]{1,0:T(8,128)(4,1)S(1)} %iota_compare_fusion), kind=kOutput, calls=%fused_computation.11 | convolution fusion | flops 2164785152 | bytes 34604032 | tf_op jit(solution)/shard_map/bkij,bkjf->bif/dot_general | solution.py:17
  156.4 0.0 copy-start.2
  156.4 0.0 copy-start
  156.4 0.0 all-gather.7.cloned.1.call-update
  156.4 0.0 all-gather.9.cloned.1.call-start
  156.5 91.1 %all-gather.7.cloned.1.call-done = bf16[4096,1024]{1,0:T(8,128)(2,1)} async-done(((bf16[4096,128]{1,0:T(8,128)(2,1)}), bf16[4096,1024]{1,0:T(8,128)(2,1)}) %all-gather.7.cloned.1.call-update) | async-done | bytes 8388624 | tf_op jit(solution)/shard_map/all_gather | solution.py:20
  247.6 0.0 copy-done.1
  247.6 0.0 copy-done.3
  247.6 7.3 %multiply_convert_fusion = (bf16[4096,128]{1,0:T(8,128)(2,1)}, bf16[4096,128]{1,0:T(8,128)(2,1)}) fusion(bf16[4096,128]{1,0:T(8,128)(2,1)S(1)} %copy-done.3, bf16[4096,1024]{1,0:T(8,128)(2,1)} %all-gather.7.cloned.1.call-done, bf16[1024,128]{1,0:T(8,128)(2,1)S(1)} %copy-done.1), kind=kOutput, calls=%fused_computation.12 | convolution fusion | flops 1080033280 | bytes 11796480 | tf_op jit(solution)/shard_map/dot_general | solution.py:19
  254.8 0.0 all-gather.9.cloned.1.call-update
  254.9 0.0 all-gather.11.cloned.1.call-start
  254.9 0.5 all-gather.11.cloned.1.call-update
  255.5 0.0 reduce-scatter.5.cloned.1.call-start
  255.5 0.0 copy-done.2
  255.5 0.1 copy.13
  255.6 0.1 reshape.58
  255.7 96.2 %all-gather.9.cloned.1.call-done = bf16[4096,1024]{1,0:T(8,128)(2,1)} async-done(((bf16[4096,128]{1,0:T(8,128)(2,1)}), bf16[4096,1024]{1,0:T(8,128)(2,1)}) %all-gather.9.cloned.1.call-update) | async-done | bytes 8388624 | tf_op jit(solution)/shard_map/all_gather | solution.py:27
  351.9 0.0 copy-done
  351.9 7.4 %convolution_convert_fusion.1 = bf16[128,1024]{0,1:T(8,128)(2,1)} fusion(bf16[4096,128]{1,0:T(8,128)(2,1)S(1)} %bitcast.24, bf16[4096,1024]{1,0:T(8,128)(2,1)} %all-gather.9.cloned.1.call-done), kind=kOutput, calls=%fused_computation.15 | convolution fusion | flops 1073872896 | bytes 9699328 | tf_op jit(solution)/shard_map/nf,nh->fh/dot_general | solution.py:28
  359.3 0.0 reduce-scatter.5.cloned.1.call-update
  359.4 0.2 reduce-scatter.3.cloned.1.call-start
  359.6 37.8 %all-gather.11.cloned.1.call-done = bf16[1024,1024]{1,0:T(8,128)(2,1)} async-done(((bf16[1024,128]{1,0:T(8,128)(2,1)}), bf16[1024,1024]{1,0:T(8,128)(2,1)}) %all-gather.11.cloned.1.call-update) | async-done | bytes 2097168 | tf_op jit(solution)/shard_map/all_gather | solution.py:32
  397.3 5.7 convolution_convert_fusion
  403.1 18.2 %fusion.3 = f32[32,16,128,128]{3,2,1,0:T(8,128)} fusion(bf16[32,128,128,1]{2,1,3,0:T(8,128)(2,1)S(1)} %bitcast.25, bf16[32,16,128,128]{3,2,1,0:T(8,128)(2,1)} %param.7, pred[32,16]{1,0:T(8,128)(4,1)S(1)} %iota_compare_fusion), kind=kOutput, calls=%fused_computation.6 | convolution fusion | flops 2155872256 | bytes 51380736 | tf_op jit(solution)/shard_map/bkij,bif->bkjf/dot_general | solution.py:39
  421.3 11.2 %broadcast_in_dim.35 = f32[512,128,128]{2,1,0:T(8,128)} broadcast(f32[]{:T(128)} %constant.9.clone.1), dimensions={} | broadcast | bytes 33554436 | tf_op jit(solution)/shard_map/broadcast_in_dim | solution.py:42
  432.5 102.6 %scatter_fusion = f32[512,128,128]{2,1,0:T(8,128)} fusion(f32[512,128,128]{2,1,0:T(8,128)} %broadcast_in_dim.35, s32[512]{0:T(512)S(1)} %reshape.58, f32[512,128,128]{2,1,0:T(8,128)} %bitcast.19), kind=kCustom, calls=%fused_computation.1 | custom fusion | flops 8388608 | bytes 100665344 | tf_op jit(solution)/shard_map/scatter-add | solution.py:42
  535.1 17.7 %convert_element_type.36 = bf16[512,128,128]{2,1,0:T(8,128)(2,1)} convert(f32[512,128,128]{2,1,0:T(8,128)} %scatter_fusion) | non-fusion elementwise | flops 8388608 | bytes 50331648 | tf_op jit(solution)/shard_map/convert_element_type | solution.py:49
  552.8 0.0 reduce-scatter.3.cloned.1.call-update
  552.8 0.0 reduce-scatter.5.cloned.1.call-done
  552.8 1.3 convert_element_type.39
  554.2 151.6 %reduce-scatter.3.cloned.1.call-done = bf16[4096,128]{1,0:T(8,128)(2,1)} async-done(((bf16[65536,128]{1,0:T(8,128)(2,1)}), bf16[4096,128]{1,0:T(8,128)(2,1)}) %reduce-scatter.3.cloned.1.call-update) | async-done | bytes 1048592 | tf_op jit(solution)/shard_map/reduce_scatter | solution.py:48
  (1 shorter events, 0.0 us)
Async XLA Ops:
  7.2 115.5 %all-gather.5.cloned.1.call-start = ((), (), s32[]{:S(2)}) async-start(), calls=%async_computation.2 | async-start | bytes 17825792 | tf_op jit(solution)/shard_map/all_gather | solution.py:12
  7.9 239.7 %all-gather.7.cloned.1.call-start = ((), (), s32[]{:S(2)}) async-start(), calls=%async_computation.3 | async-start | bytes 9437184 | tf_op jit(solution)/shard_map/all_gather | solution.py:20
  142.3 105.3 %copy-start.1 = (bf16[1024,128]{1,0:T(8,128)(2,1)S(1)}, bf16[1024,128]{1,0:T(8,128)(2,1)}, u32[]{:S(2)}) copy-start(bf16[1024,128]{1,0:T(8,128)(2,1)} %param.10) | copy-start | bytes 786436
  142.3 105.3 %copy-start.3 = (bf16[4096,128]{1,0:T(8,128)(2,1)S(1)}, bf16[4096,128]{1,0:T(8,128)(2,1)}, u32[]{:S(2)}) copy-start(bf16[4096,128]{1,0:T(8,128)(2,1)} %param.11) | copy-start | bytes 3145732
  156.4 99.1 %copy-start.2 = (s32[32,16]{0,1:T(8,128)S(1)}, s32[32,16]{0,1:T(8,128)}, u32[]{:S(2)}) copy-start(s32[32,16]{0,1:T(8,128)} %param.8) | copy-start | bytes 6148
  156.4 195.5 %copy-start = (bf16[32,128,128]{2,1,0:T(8,128)(2,1)S(1)}, bf16[32,128,128]{2,1,0:T(8,128)(2,1)}, u32[]{:S(2)}) copy-start(bf16[32,128,128]{2,1,0:T(8,128)(2,1)} %bitcast_convert_fusion) | copy-start | bytes 3145732
  156.4 195.4 %all-gather.9.cloned.1.call-start = ((), (), s32[]{:S(2)}) async-start(), calls=%async_computation.4 | async-start | bytes 9437184 | tf_op jit(solution)/shard_map/all_gather | solution.py:27
  254.9 142.5 %all-gather.11.cloned.1.call-start = ((), (), s32[]{:S(2)}) async-start(), calls=%async_computation.5 | async-start | bytes 2359296 | tf_op jit(solution)/shard_map/all_gather | solution.py:32
  255.5 297.4 %reduce-scatter.5.cloned.1.call-start = ((), (), s32[]{:S(2)}) async-start(), calls=%async_computation.7 | async-start | bytes 278528 | tf_op jit(solution)/shard_map/reduce_scatter | solution.py:29
  359.4 346.4 %reduce-scatter.3.cloned.1.call-start = ((), (), s32[]{:S(2)}) async-start(), calls=%async_computation.6 | async-start | bytes 17825792 | tf_op jit(solution)/shard_map/reduce_scatter | solution.py:48
Sparse Core Ops, SparseCore 0:
  10.4 112.1 all-gather.4
  156.6 90.9 all-gather.6
  255.0 96.8 all-gather.8
  353.3 43.9 all-gather.10
  400.9 69.1 reduce-scatter.4
  552.9 152.8 reduce-scatter.2
where the time goes:
time: 714 us; the launch traced here: 713 us
  waiting for transfers between devices  490 us (69%)
  other arithmetic  124 us (17%)
  matrix products  52.8 us (7%)
  local copies, waits for them, and re-layouts  31.3 us (4%)
  between operations  14.1 us (2%)
    reduce_scatter x1, waiting for transfers between devices, local(): lax.psum_scatter(scattered.astype(jnp.bfloat16), 'row', scatter_dimension...  152 us
    all_gather x1, waiting for transfers between devices, local(): gathered = lax.all_gather(features, 'row', axis=0, tiled=True)  112 us
    scatter-add x1, other arithmetic, local(): jax.ops.segment_sum(contrib.reshape(blocks_here * slots, tile_size, feat_...  103 us
    all_gather x1, waiting for transfers between devices, local(): grad_cols = lax.all_gather(grad_out, 'rep', axis=1, tiled=True)  96.2 us
    all_gather x1, waiting for transfers between devices, local(): lax.all_gather(mixed, 'rep', axis=1, tiled=True)  91.1 us
    all_gather x1, waiting for transfers between devices, local(): full_weight = lax.all_gather(weight, 'rep', axis=1, tiled=True)  37.8 us
    gather x1, local copies, waits for them, and re-layouts, local(): operand = jnp.take(source_blocks, columns, axis=0)  19.6 us
    dot_general x1, matrix products, local(): jnp.einsum('bkij,bif->bkjf', masked_tiles, grad_blocks, preferred_element...  18.2 us
  transfers between devices with their start and end apart: 6, of which 5 were waited for; matrix products, arithmetic and copies ran while one was open for 23% of the time, Pallas kernels for 0%

commit v1 on v0

v1 whole, which is shorter than its diff:
```python
import functools

import jax
import jax.numpy as jnp
from jax import lax
from jax.experimental import pallas as pl
from jax.experimental.pallas import tpu as pltpu
from jax.sharding import PartitionSpec as P

F32 = jnp.float32
BF16 = jnp.bfloat16
SLOTS_AHEAD = 4


def fwd_kernel(cols, counts, tiles, gathered, out, tbuf, gbuf, sems):
    blocks, slots, t, _ = tiles.shape

    def copies(b, k):
        s = lax.rem(b, SLOTS_AHEAD)
        at = pl.ds(pl.multiple_of(k * t, t), t)
        return (
            pltpu.make_async_copy(tiles.at[b, k], tbuf.at[s, :, at], sems.at[s, k, 0]),
            pltpu.make_async_copy(gathered.at[cols[b, k]], gbuf.at[s, at, :], sems.at[s, k, 1]),
        )

    def start(b):
        @pl.loop(0, counts[b])
        def _(k):
            for c in copies(b, k):
                c.start()

    for b in range(SLOTS_AHEAD - 1):
        start(b)

    @pl.loop(0, blocks)
    def _(b):
        s = lax.rem(b, SLOTS_AHEAD)

        @pl.when(b + SLOTS_AHEAD - 1 < blocks)
        def _():
            start(b + SLOTS_AHEAD - 1)

        n = counts[b]

        @pl.loop(0, n)
        def _(k):
            for c in copies(b, k):
                c.wait()

        @pl.when(lax.rem(n, 2) == 1)
        def _():
            at = pl.ds(pl.multiple_of(n * t, t), t)
            tbuf[s, :, at] = jnp.zeros((t, t), BF16)
            gbuf[s, at, :] = jnp.zeros((t, t), BF16)

        row = pl.ds(pl.multiple_of(b * t, t), t)
        for p in range(1, slots // 2 + 1):

            @pl.when((n + 1) // 2 == p)
            def _():
                w = 2 * p * t
                out[row, :] = jnp.dot(
                    tbuf[s, :, :w], gbuf[s, :w, :], preferred_element_type=F32
                ).astype(BF16)


def spmm(gathered, tiles, columns, counts):
    blocks, slots, t, _ = tiles.shape
    width = gathered.shape[-1]
    return pl.pallas_call(
        fwd_kernel,
        grid_spec=pltpu.PrefetchScalarGridSpec(
            num_scalar_prefetch=2,
            grid=(1,),
            in_specs=[pl.BlockSpec(memory_space=pl.ANY)] * 2,
            out_specs=pl.BlockSpec((blocks * t, width), lambda i, *_: (0, 0)),
            scratch_shapes=[
                pltpu.VMEM((SLOTS_AHEAD, t, slots * t), BF16),
                pltpu.VMEM((SLOTS_AHEAD, slots * t, width), BF16),
                pltpu.SemaphoreType.DMA((SLOTS_AHEAD, slots, 2)),
            ],
        ),
        out_shape=jax.ShapeDtypeStruct((blocks * t, width), BF16),
        name="spmm",
    )(columns, counts, tiles, gathered)


GROUP = 4
OUT_CHUNK = 16


def bwd_kernel(cols, counts, tiles, grad, out, acc, tbuf, stage, sems, out_sems):
    blocks, slots, t, _ = tiles.shape
    total = acc.shape[0]

    def copy(b, k):
        s = lax.rem(b, SLOTS_AHEAD)
        return pltpu.make_async_copy(tiles.at[b, k], tbuf.at[s, k], sems.at[s, k])

    def start(b):
        @pl.loop(0, counts[b])
        def _(k):
            copy(b, k).start()

    for b in range(SLOTS_AHEAD - 1):
        start(b)

    @pl.loop(0, total)
    def _(j):
        acc[j] = jnp.zeros(acc.shape[1:], F32)

    @pl.loop(0, blocks)
    def _(b):
        s = lax.rem(b, SLOTS_AHEAD)

        @pl.when(b + SLOTS_AHEAD - 1 < blocks)
        def _():
            start(b + SLOTS_AHEAD - 1)

        n = counts[b]

        @pl.loop(0, n)
        def _(k):
            copy(b, k).wait()

        g = grad[pl.ds(pl.multiple_of(b * t, t), t), :]

        @pl.loop(0, (n + GROUP - 1) // GROUP)
        def _(q):
            terms = []
            for i in range(GROUP):
                k = q * GROUP + i
                term = lax.dot_general(
                    tbuf[s, k], g, (((0,), (0,)), ((), ())), preferred_element_type=F32
                )
                terms.append(jnp.where(k < n, term, 0.0))
            for i in range(GROUP):
                acc[cols[b, q * GROUP + i]] += terms[i]

    def flush(c):
        s = lax.rem(c, 2)
        return pltpu.make_async_copy(
            stage.at[s], out.at[pl.ds(c * OUT_CHUNK, OUT_CHUNK)], out_sems.at[s]
        )

    @pl.loop(0, total // OUT_CHUNK)
    def _(c):
        s = lax.rem(c, 2)

        @pl.when(c >= 2)
        def _():
            flush(c - 2).wait()

        @pl.loop(0, OUT_CHUNK)
        def _(j):
            stage[s, j] = acc[c * OUT_CHUNK + j].astype(BF16)

        flush(c).start()

    for c in (total // OUT_CHUNK - 2, total // OUT_CHUNK - 1):
        flush(c).wait()


def spmm_t(grad, tiles, columns, counts, total):
    blocks, slots, t, _ = tiles.shape
    width = grad.shape[-1]
    return pl.pallas_call(
        bwd_kernel,
        grid_spec=pltpu.PrefetchScalarGridSpec(
            num_scalar_prefetch=2,
            grid=(1,),
            in_specs=[
                pl.BlockSpec(memory_space=pl.ANY),
                pl.BlockSpec((blocks * t, width), lambda i, *_: (0, 0)),
            ],
            out_specs=pl.BlockSpec(memory_space=pl.ANY),
            scratch_shapes=[
                pltpu.VMEM((total, t, width), F32),
                pltpu.VMEM((SLOTS_AHEAD, slots, t, t), BF16),
                pltpu.VMEM((2, OUT_CHUNK, t, width), BF16),
                pltpu.SemaphoreType.DMA((SLOTS_AHEAD, slots)),
                pltpu.SemaphoreType.DMA((2,)),
            ],
        ),
        out_shape=jax.ShapeDtypeStruct((total, t, width), BF16),
        compiler_params=pltpu.CompilerParams(vmem_limit_bytes=60 * 1024 * 1024),
        name="spmm_t",
    )(columns, counts, tiles, grad)


def local(features, tiles, columns, counts, weight, cotangent):
    rows_here, feat_local = features.shape
    blocks_here, slots, t, _ = tiles.shape
    total_blocks = blocks_here * lax.axis_size("row")
    gathered = lax.all_gather(features, "row", axis=0, tiled=True)
    cot = lax.all_to_all(cotangent, "rep", 0, 1, tiled=True)
    w = lax.all_gather(weight, "rep", axis=1, tiled=True)
    mixed = spmm(gathered.reshape(total_blocks, t, feat_local), tiles, columns, counts)
    mixed = lax.all_to_all(mixed, "rep", 0, 1, tiled=True)
    preact = jnp.dot(mixed, w, preferred_element_type=F32)
    sig = jax.nn.sigmoid(preact)
    act = (preact * sig).astype(BF16)
    activations = lax.all_to_all(act, "rep", 1, 0, tiled=True)
    grad_out = (cot.astype(F32) * sig * (1.0 + preact * (1.0 - sig))).astype(BF16)
    mixed_grad = lax.dot_general(
        grad_out, w, (((1,), (1,)), ((), ())), preferred_element_type=F32
    ).astype(BF16)
    mixed_grad = lax.all_to_all(mixed_grad, "rep", 1, 0, tiled=True)
    terms = lax.dot_general(mixed, grad_out, (((0,), (0,)), ((), ())), preferred_element_type=F32)
    terms = lax.psum_scatter(terms.astype(BF16), "rep", scatter_dimension=0, tiled=True)
    weight_grad = lax.psum_scatter(terms, "row", scatter_dimension=1, tiled=True).astype(F32)
    partial = spmm_t(mixed_grad, tiles, columns, counts, total_blocks)
    feature_grad = lax.psum_scatter(
        partial.reshape(total_blocks * t, feat_local), "row", scatter_dimension=0, tiled=True
    )
    return activations, feature_grad, weight_grad


def solution(mesh):
    in_specs = (
        P("row", "rep"),
        P("row", None, None, None),
        P("row", None),
        P("row"),
        P(None, "rep"),
        P("row", "rep"),
    )
    out_specs = (P("row", "rep"), P("row", "rep"), P("rep", "row"))
    return jax.shard_map(local, mesh=mesh, in_specs=in_specs, out_specs=out_specs, check_vma=False)
```

time: 714 us -> 464 us (0.65)
  waiting for transfers between devices: 490 us -> 335 us
  other arithmetic: 124 us -> 0 us
  Pallas kernels: 0 us -> 63.7 us
  matrix products: 52.8 us -> 8.75 us
  local copies, waits for them, and re-layouts: 31.3 us -> 12.1 us
  starting transfers between devices: 0.42 us -> 16.4 us
  blocking collectives: 0 us -> 13.3 us
    all_gather x3 -> x1, waiting for transfers between devices: 225 us -> 22.1 us  [local(): w = lax.all_gather(weight, 'rep', axis=1, tiled=True)]
    scatter-add x1 -> x0, other arithmetic: 103 us -> none  [local(): jax.ops.segment_sum(contrib.reshape(blocks_here * slots, tile_size, feat_...]
    pallas_call x0 -> x2, Pallas kernels: none -> 63.7 us  [the longest x1 44.2 us: spmm_t(): pl.pallas_call(bwd_kernel, grid_spec=pltpu.PrefetchScalarGridSpec(num_sca...]
    dot_general x5 -> x3, matrix products: 52.8 us -> 8.75 us  [the longest x1 3.63 us: local(): preact = jnp.dot(mixed, w, preferred_element_type=F32)]
    reduce_scatter x2, waiting for transfers between devices: 152 us -> 191 us  [the longest x1 151 us: local(): lax.psum_scatter(partial.reshape(total_blocks * t, feat_local), 'row', sc...]
    gather x1 -> x0, local copies, waits for them, and re-layouts: 19.6 us -> none  [local(): operand = jnp.take(source_blocks, columns, axis=0)]
    convert_element_type x2 -> x0, other arithmetic: 19 us -> none  [the longest x1 17.7 us: local(): scattered.astype(jnp.bfloat16)]
    all_to_all x0 -> x3, starting transfers between devices: none -> 16.2 us  [the longest x1 6.79 us: local(): cot = lax.all_to_all(cotangent, 'rep', 0, 1, tiled=True)]
  transfers between devices with their start and end apart: 6 -> 8, of which waited for: 5 -> 5; matrix products, arithmetic and copies ran while one was open for 23% -> 2% of each run, Pallas kernels for 0% -> 14%
where the time goes in v1:
time: 464 us
  waiting for transfers between devices  335 us (72%)
  Pallas kernels  63.7 us (14%)
  starting transfers between devices  16.4 us (4%)
  between operations  13.9 us (3%)
  blocking collectives  13.3 us (3%)
  local copies, waits for them, and re-layouts  12.1 us (3%)
  matrix products  8.75 us (2%)
    reduce_scatter x1, waiting for transfers between devices, local(): lax.psum_scatter(partial.reshape(total_blocks * t, feat_local), 'row', sc...  151 us
    all_gather x1, waiting for transfers between devices, local(): gathered = lax.all_gather(features, 'row', axis=0, tiled=True)  110 us
    pallas_call x1, Pallas kernels, spmm_t(): pl.pallas_call(bwd_kernel, grid_spec=pltpu.PrefetchScalarGridSpec(num_sca...  44.2 us
    reduce_scatter x1, waiting for transfers between devices, local(): lax.psum_scatter(terms.astype(BF16), 'rep', scatter_dimension=0, tiled=True)  40.2 us
    all_gather x1, waiting for transfers between devices, local(): w = lax.all_gather(weight, 'rep', axis=1, tiled=True)  22.1 us
    pallas_call x1, Pallas kernels, spmm(): pl.pallas_call(fwd_kernel, grid_spec=pltpu.PrefetchScalarGridSpec(num_sca...  19.6 us
    all_to_all x1, blocking collectives, local(): activations = lax.all_to_all(act, 'rep', 1, 0, tiled=True)  13.3 us
    unnamed x6, waiting for transfers between devices  12.6 us
  transfers between devices with their start and end apart: 8, of which 5 were waited for; matrix products, arithmetic and copies ran while one was open for 2% of the time, Pallas kernels for 14%

profile of v1, /device:TPU:1, one launch (start us, length us, event | category | flops | bytes accessed | tf_op | source)
XLA Modules:
  0.0 463.5 jit_solution(16479545777114642408)
XLA Ops:
  7.2 0.0 copy-start.1
  7.2 0.0 all-gather.3.cloned.1.call-start
  7.2 0.7 all-gather.3.cloned.1.call-update
  7.9 0.0 all-gather.5.cloned.1.call-start
  8.0 0.7 all-gather.5.cloned.1.call-update
  8.7 6.8 %all-to-all-start.2 = ((bf16[8,512,128]{2,1,0:T(8,128)(2,1)}), bf16[8,512,128]{2,1,0:T(8,128)(2,1)S(1)}, u32[]{:S(2)}, u32[]{:S(2)}) async-start(bf16[8,512,128]{2,1,0:T(8,128)(2,1)} %bitcast.47), calls=%async_computation.2 | async-start | bytes 2097152 | tf_op jit(solution)/shard_map/all_to_all | solution.py:196
  15.4 0.0 copy-done.1
  15.5 0.7 copy.22.cols
  16.1 109.7 %all-gather.3.cloned.1.call-done = bf16[65536,128]{1,0:T(8,128)(2,1)} async-done(((bf16[4096,128]{1,0:T(8,128)(2,1)}), bf16[65536,128]{1,0:T(8,128)(2,1)}) %all-gather.3.cloned.1.call-update) | async-done | bytes 16777232 | tf_op jit(solution)/shard_map/all_gather | solution.py:195
  125.8 19.6 %spmm.1 = bf16[4096,128]{1,0:T(8,128)(2,1)} custom-call(s32[32,16]{1,0:T(8,128)} %copy.22.cols, s32[32]{0:T(128)} %counts.3, bf16[32,16,128,128]{3,2,1,0:T(8,128)(2,1)} %tiles.3, bf16[512,128,128]{2,1,0:T(8,128)(2,1)} %bitcast.42), custom_call_target="tpu_custom_call" | custom-call | tf_op jit(solution)/shard_map/spmm/pallas_call | solution.py:70
  145.4 2.3 copy.23
  147.6 0.0 all-to-all-done.2
  147.6 4.1 all-to-all-start
  151.8 0.0 reduce-scatter.8.cloned.1.call-start
  151.8 22.1 %all-gather.5.cloned.1.call-done = bf16[1024,1024]{1,0:T(8,128)(2,1)} async-done(((bf16[1024,128]{1,0:T(8,128)(2,1)}), bf16[1024,1024]{1,0:T(8,128)(2,1)}) %all-gather.5.cloned.1.call-update) | async-done | bytes 2097168 | tf_op jit(solution)/shard_map/all_gather | solution.py:197
  173.9 0.0 all-to-all-done
  173.9 3.6 fusion.1
  177.5 0.0 copy-start.3
  177.6 1.0 copy-done.3
  178.5 2.6 convolution_convert_fusion
  181.1 0.0 copy-start.2
  181.1 0.0 reduce-scatter.8.cloned.1.call-update
  181.2 1.6 copy-done.2
  182.7 2.5 fusion.2
  185.2 1.2 copy.37
  186.4 5.3 %all-to-all-start.3 = ((bf16[512,8,128]{2,0,1:T(8,128)(2,1)}), bf16[512,8,128]{2,0,1:T(8,128)(2,1)S(1)}, u32[]{:S(2)}, u32[]{:S(2)}) async-start(bf16[512,8,128]{2,0,1:T(8,128)(2,1)} %bitcast.39), calls=%async_computation.3 | async-start | bytes 2097152 | tf_op jit(solution)/shard_map/all_to_all | solution.py:208
  191.7 0.0 reduce-scatter.10.cloned.1.call-start
  191.8 40.2 %reduce-scatter.8.cloned.1.call-done = bf16[128,1024]{1,0:T(8,128)(2,1)} async-done(((bf16[1024,1024]{1,0:T(8,128)(2,1)}), bf16[128,1024]{1,0:T(8,128)(2,1)}) %reduce-scatter.8.cloned.1.call-update) | async-done | bytes 262160 | tf_op jit(solution)/shard_map/reduce_scatter | solution.py:210
  231.9 1.8 copy.29
  233.7 0.0 reduce-scatter.10.cloned.1.call-update
  233.7 0.0 reduce-scatter.6.cloned.1.call-start
  233.8 0.0 all-to-all-done.3
  233.8 0.0 copy-start
  233.8 1.0 copy-done
  234.7 44.2 %spmm_t.1 = bf16[512,128,128]{2,1,0:T(8,128)(2,1)} custom-call(s32[32,16]{1,0:T(8,128)} %copy.22.cols, s32[32]{0:T(128)} %counts.3, bf16[32,16,128,128]{3,2,1,0:T(8,128)(2,1)} %tiles.3, bf16[4096,128]{1,0:T(8,128)(2,1)} %bitcast.43), custom_call_target="tpu_custom_call" | custom-call | tf_op jit(solution)/shard_map/spmm_t/pallas_call | solution.py:167
  278.9 0.0 reduce-scatter.6.cloned.1.call-update
  279.0 0.2 copy.38
  279.2 13.3 %all_to_all.70 = bf16[512,8,128]{2,0,1:T(8,128)(2,1)S(1)} all-to-all(bf16[512,8,128]{2,0,1:T(8,128)(2,1)S(1)} %bitcast.46), channel_id=1, replica_groups=mesh['row'=16,'rep'=8] {'rep'}, dimensions={1} | all-to-all | bytes 2097152 | tf_op jit(solution)/shard_map/all_to_all | solution.py:203
  292.4 11.2 %reduce-scatter.10.cloned.1.call-done = bf16[64,128]{1,0:T(8,128)(2,1)} async-done(((bf16[1024,128]{1,0:T(8,128)(2,1)}), bf16[64,128]{1,0:T(8,128)(2,1)}) %reduce-scatter.10.cloned.1.call-update) | async-done | bytes 16400
  303.6 0.8 copy.30
  304.4 0.7 copy.28
  305.2 150.8 %reduce-scatter.6.cloned.1.call-done = bf16[4096,128]{1,0:T(8,128)(2,1)} async-done(((bf16[65536,128]{1,0:T(8,128)(2,1)}), bf16[4096,128]{1,0:T(8,128)(2,1)}) %reduce-scatter.6.cloned.1.call-update) | async-done | bytes 1048592 | tf_op jit(solution)/shard_map/reduce_scatter | solution.py:213
  456.0 1.0 copy.40
Async XLA Ops:
  7.2 8.3 %copy-start.1 = (s32[32,16]{0,1:T(8,128)S(1)}, s32[32,16]{0,1:T(8,128)}, u32[]{:S(2)}) copy-start(s32[32,16]{0,1:T(8,128)} %param.8) | copy-start | bytes 6148
  7.2 118.6 %all-gather.3.cloned.1.call-start = ((), (), s32[]{:S(2)}) async-start(), calls=%async_computation.7 | async-start | bytes 17825792 | tf_op jit(solution)/shard_map/all_gather | solution.py:195
  7.9 166.0 %all-gather.5.cloned.1.call-start = ((), (), s32[]{:S(2)}) async-start(), calls=%async_computation.8 | async-start | bytes 2359296 | tf_op jit(solution)/shard_map/all_gather | solution.py:197
  8.7 139.0 %all-to-all-start.2 = ((bf16[8,512,128]{2,1,0:T(8,128)(2,1)}), bf16[8,512,128]{2,1,0:T(8,128)(2,1)S(1)}, u32[]{:S(2)}, u32[]{:S(2)}) async-start(bf16[8,512,128]{2,1,0:T(8,128)(2,1)} %bitcast.47), calls=%async_computation.2 | async-start | bytes 2097152 | tf_op jit(solution)/shard_map/all_to_all | solution.py:196
  147.6 26.3 %all-to-all-start = ((bf16[8,512,128]{1,2,0:T(8,128)(2,1)}), bf16[8,512,128]{1,2,0:T(8,128)(2,1)S(1)}, u32[]{:S(2)}, u32[]{:S(2)}) async-start(bf16[8,512,128]{1,2,0:T(8,128)(2,1)} %copy.23), calls=%async_computation | async-start | bytes 2097152 | tf_op jit(solution)/shard_map/all_to_all | solution.py:199
  151.8 80.1 %reduce-scatter.8.cloned.1.call-start = ((), (), s32[]{:S(2)}) async-start(), calls=%async_computation.10 | async-start | bytes 2359296 | tf_op jit(solution)/shard_map/reduce_scatter | solution.py:210
  177.5 1.0 copy-start.3
  181.1 1.6 copy-start.2
  186.4 47.4 %all-to-all-start.3 = ((bf16[512,8,128]{2,0,1:T(8,128)(2,1)}), bf16[512,8,128]{2,0,1:T(8,128)(2,1)S(1)}, u32[]{:S(2)}, u32[]{:S(2)}) async-start(bf16[512,8,128]{2,0,1:T(8,128)(2,1)} %bitcast.39), calls=%async_computation.3 | async-start | bytes 2097152 | tf_op jit(solution)/shard_map/all_to_all | solution.py:208
  191.7 111.9 %reduce-scatter.10.cloned.1.call-start = ((), (), s32[]{:S(2)}) async-start(), calls=%async_computation.11 | async-start | bytes 278528
  233.7 222.3 %reduce-scatter.6.cloned.1.call-start = ((), (), s32[]{:S(2)}) async-start(), calls=%async_computation.9 | async-start | bytes 17825792 | tf_op jit(solution)/shard_map/reduce_scatter | solution.py:213
  233.8 1.0 copy-start
Sparse Core Ops, SparseCore 0:
  10.4 115.3 all-gather.2
  127.4 46.4 all-gather.4
  181.3 50.5 reduce-scatter.7
  236.0 67.5 reduce-scatter.9
  308.3 147.6 reduce-scatter.5

commit v2 on v1

--- a/solution.py
+++ b/solution.py
@@ -9,6 +9,221 @@
 
 F32 = jnp.float32
 BF16 = jnp.bfloat16
+MESH = pl.DeviceIdType.MESH
+ROWS_Y = 4
+N_ROW = 16
+N_REP = 8
+ANY = pl.BlockSpec(memory_space=pl.ANY)
+VM = pl.BlockSpec(memory_space=pltpu.VMEM)
+
+
+class Place:
+    def __init__(self):
+        self.row = lax.axis_index("row")
+        self.rep = lax.axis_index("rep")
+        self.c = lax.rem(self.row, 2)
+        self.y = lax.rem(self.row // 2, ROWS_Y)
+        self.h = self.row // (2 * ROWS_Y)
+
+    def slot(self, other, dy, sib=False):
+        h = 1 - self.h if other else self.h
+        c = 1 - self.c if sib else self.c
+        return (h * ROWS_Y + lax.rem(self.y + dy + ROWS_Y, ROWS_Y)) * 2 + c
+
+    def at(self, other, dy, sib=False):
+        return (self.slot(other, dy, sib), self.rep)
+
+    def peer(self, d):
+        x, z = self.rep // 4, lax.rem(self.rep, 4)
+        if d >= 4:
+            x = 1 - x
+        if d % 4 == 1:
+            z = z + 1 - 2 * lax.rem(z, 2)
+        elif d % 4 == 2:
+            z = lax.rem(z + 2, 4)
+        elif d % 4 == 3:
+            z = 3 - z
+        return x * 4 + z
+
+
+def greet(partners):
+    barrier = pltpu.get_barrier_semaphore()
+    for partner in partners:
+        pl.semaphore_signal(barrier, inc=1, device_id=partner, device_id_type=MESH)
+    pl.semaphore_wait(barrier, len(partners))
+
+
+class Sends:
+    def __init__(self, sems):
+        self.sems, self.live = sems, []
+
+    def __call__(self, src, dst, recv_sem, device):
+        copy = pltpu.make_async_remote_copy(
+            src_ref=src,
+            dst_ref=dst,
+            send_sem=self.sems.at[len(self.live)],
+            recv_sem=recv_sem,
+            device_id=device,
+            device_id_type=MESH,
+        )
+        copy.start()
+        self.live.append(copy)
+
+    def finish(self):
+        for copy in self.live:
+            copy.wait_send()
+
+
+def arrived(dst, recv_sem):
+    pltpu.make_async_copy(dst, dst, recv_sem).wait()
+
+
+CHUNKS = 4
+
+
+def gather_kernel(
+    feats, cot, weight, gathered, cots, ws, own, own_w, own_c,
+    send_sems, recv_sems, cot_recv, w_recv, w_sib, local_sems,
+):
+    here = Place()
+    step = feats.shape[0] // CHUNKS
+    piece = cot.shape[0] // N_REP
+    half = weight.shape[0] // 2
+    peers = [here.peer(d) for d in range(1, N_REP)]
+    sib = here.at(False, 0, True)
+    up, down, across = here.at(False, 1), here.at(False, -1), here.at(True, 0)
+
+    loads = [
+        pltpu.make_async_copy(feats, own, local_sems.at[0]),
+        pltpu.make_async_copy(weight, own_w, local_sems.at[1]),
+        pltpu.make_async_copy(
+            cot.at[pl.ds(pl.multiple_of(here.rep * piece, piece), piece)], own_c, local_sems.at[2]
+        ),
+    ]
+    for load in loads:
+        load.start()
+    greet([sib, up, down, across] + [(here.row, q) for q in peers])
+
+    send = Sends(send_sems)
+
+    def rows(chunk):
+        return pl.ds(chunk * step, step)
+
+    def place(slot, chunk):
+        return gathered.at[slot, rows(chunk)]
+
+    slots = [
+        here.slot(False, -1), here.slot(False, 1), here.slot(False, 2), here.slot(True, 0),
+        here.slot(True, -1), here.slot(True, 1), here.slot(True, 2),
+    ]
+
+    def launch(src_of, slot, order, base, to_x, sib_kind):
+        for i in range(CHUNKS):
+            if to_x:
+                send(src_of(i), place(slot, i), recv_sems.at[3, i], across)
+        for i in range(CHUNKS):
+            a, b = i, (i + CHUNKS // 2) % CHUNKS
+            send(src_of(a), place(slot, a), recv_sems.at[base, a], up)
+            send(src_of(b), place(slot, b), recv_sems.at[base + 1, b], down)
+        for i in range(CHUNKS):
+            send(src_of(i), place(slot, i), recv_sems.at[sib_kind, i], sib)
+
+    launch(lambda i: feats.at[rows(i)], here.row, None, 0, True, 7)
+
+    mine = pl.ds(pl.multiple_of(here.c * half, half), half)
+    for d in range(1, N_REP):
+        q = peers[d - 1]
+        send(weight.at[mine], ws.at[here.rep, mine], w_recv.at[d - 1], (here.row, q))
+    for d in range(1, N_REP):
+        q = peers[d - 1]
+        send(
+            cot.at[pl.ds(pl.multiple_of(q * piece, piece), piece)],
+            cots.at[here.rep], cot_recv.at[d - 1], (here.row, q),
+        )
+
+    stores = [
+        pltpu.make_async_copy(own, gathered.at[here.row], local_sems.at[3]),
+        pltpu.make_async_copy(own_w, ws.at[here.rep], local_sems.at[4]),
+        pltpu.make_async_copy(own_c, cots.at[here.rep], local_sems.at[5]),
+    ]
+    for load, store in zip(loads, stores):
+        load.wait()
+        store.start()
+
+    def take(kind, chunk, to_up, to_down):
+        slot = slots[kind]
+        arrived(place(slot, chunk), recv_sems.at[kind, chunk])
+        far = 2 if kind < 3 else 6
+        if to_up:
+            send(place(slot, chunk), place(slot, chunk), recv_sems.at[far, chunk], up)
+        if to_down:
+            send(place(slot, chunk), place(slot, chunk), recv_sems.at[far, chunk], down)
+        send(place(slot, chunk), place(slot, chunk), recv_sems.at[8 + kind, chunk], sib)
+
+    for base in (0, 4):
+        for i in range(CHUNKS):
+            a, b = i, (i + CHUNKS // 2) % CHUNKS
+            take(base, a, a < CHUNKS // 2, False)
+            take(base + 1, b, False, b >= CHUNKS // 2)
+            if base == 0:
+                arrived(place(slots[3], i), recv_sems.at[3, i])
+                src = place(slots[3], i)
+                send(src, src, recv_sems.at[4, i], up)
+                send(src, src, recv_sems.at[5, i], down)
+                send(src, src, recv_sems.at[11, i], sib)
+        for i in range(CHUNKS):
+            take(2 if base == 0 else 6, i, False, False)
+        if base == 0:
+            for d in range(1, N_REP):
+                q = peers[d - 1]
+                arrived(ws.at[q, mine], w_recv.at[d - 1])
+                send(ws.at[q, mine], ws.at[q, mine], w_sib.at[d - 1], sib)
+
+    theirs = pl.ds(pl.multiple_of((1 - here.c) * half, half), half)
+    for d in range(1, N_REP):
+        q = peers[d - 1]
+        arrived(ws.at[q, theirs], w_sib.at[d - 1])
+        arrived(cots.at[q], cot_recv.at[d - 1])
+    sib_slots = [here.slot(False, 0, True)] + [
+        here.slot(other, dy, True)
+        for other, dy in ((False, -1), (False, 1), (False, 2), (True, 0), (True, -1), (True, 1), (True, 2))
+    ]
+    for kind in range(8):
+        for i in range(CHUNKS):
+            arrived(place(sib_slots[kind], i), recv_sems.at[7 + kind, i])
+    for store in stores:
+        store.wait()
+    send.finish()
+
+
+def gather_all(features, cotangent, weight):
+    rows, width = features.shape
+    n_sends = 15 * CHUNKS + 21
+    return pl.pallas_call(
+        gather_kernel,
+        in_specs=[ANY] * 3,
+        out_specs=[ANY] * 3,
+        out_shape=[
+            jax.ShapeDtypeStruct((N_ROW, rows, width), BF16),
+            jax.ShapeDtypeStruct((N_REP, rows // N_REP, width), BF16),
+            jax.ShapeDtypeStruct((N_REP,) + weight.shape, BF16),
+        ],
+        scratch_shapes=[
+            pltpu.VMEM((rows, width), BF16),
+            pltpu.VMEM(weight.shape, BF16),
+            pltpu.VMEM((rows // N_REP, width), BF16),
+            pltpu.SemaphoreType.DMA((n_sends,)),
+            pltpu.SemaphoreType.DMA((15, CHUNKS)),
+            pltpu.SemaphoreType.DMA((N_REP - 1,)),
+            pltpu.SemaphoreType.DMA((N_REP - 1,)),
+            pltpu.SemaphoreType.DMA((N_REP - 1,)),
+            pltpu.SemaphoreType.DMA((6,)),
+        ],
+        compiler_params=pltpu.CompilerParams(collective_id=0, has_side_effects=True),
+        name="gather_all",
+    )(features, cotangent, weight)
+
+
 SLOTS_AHEAD = 4
 
 
@@ -192,9 +407,9 @@
     rows_here, feat_local = features.shape
     blocks_here, slots, t, _ = tiles.shape
     total_blocks = blocks_here * lax.axis_size("row")
-    gathered = lax.all_gather(features, "row", axis=0, tiled=True)
-    cot = lax.all_to_all(cotangent, "rep", 0, 1, tiled=True)
-    w = lax.all_gather(weight, "rep", axis=1, tiled=True)
+    gathered, cot, w = gather_all(features, cotangent, weight)
+    cot = jnp.swapaxes(cot, 0, 1).reshape(-1, N_REP * feat_local)
+    w = jnp.swapaxes(w, 0, 1).reshape(-1, N_REP * feat_local)
     mixed = spmm(gathered.reshape(total_blocks, t, feat_local), tiles, columns, counts)
     mixed = lax.all_to_all(mixed, "rep", 0, 1, tiled=True)
     preact = jnp.dot(mixed, w, preferred_element_type=F32)

time: 464 us -> 417 us (0.90)
  waiting for transfers between devices: 335 us -> 204 us
  Pallas kernels: 63.7 us -> 147 us
  starting transfers between devices: 16.4 us -> 7.99 us
  local copies, waits for them, and re-layouts: 12.1 us -> 18.9 us
    all_gather x2 -> x0, waiting for transfers between devices: 132 us -> none  [the longest x1 110 us: local(): gathered = lax.all_gather(features, 'row', axis=0, tiled=True)]
    pallas_call x0 -> x1, Pallas kernels: none -> 81.4 us  [gather_all(): pl.pallas_call(gather_kernel, in_specs=[ANY] * 3, out_specs=[ANY] * 3, ou...]
    all_to_all x1, waiting for transfers between devices: 0.01 us -> 7.23 us  [local(): mixed = lax.all_to_all(mixed, 'rep', 0, 1, tiled=True)]
    all_to_all x1 -> x0, starting transfers between devices: 6.79 us -> none  [local(): cot = lax.all_to_all(cotangent, 'rep', 0, 1, tiled=True)]
    convert_element_type x0 -> x2, local copies, waits for them, and re-layouts: none -> 4.9 us  [local(): cot.astype(F32) * sig * (1.0 + preact * (1.0 - sig))]
    unnamed x6 -> x4, waiting for transfers between devices: 12.6 us -> 8.85 us
  transfers between devices with their start and end apart: 8 -> 5, of which waited for: 5 -> 4; matrix products, arithmetic and copies ran while one was open for 2% -> 4% of each run, Pallas kernels for 14% -> 11%
where the time goes in v2:
time: 417 us; the launch traced here: 416 us
  waiting for transfers between devices  204 us (49%)
  Pallas kernels  147 us (35%)
  local copies, waits for them, and re-layouts  18.9 us (5%)
  between operations  13.9 us (3%)
  blocking collectives  13.6 us (3%)
  matrix products  10.2 us (2%)
  starting transfers between devices  7.99 us (2%)
    reduce_scatter x1, waiting for transfers between devices, local(): lax.psum_scatter(partial.reshape(total_blocks * t, feat_local), 'row', sc...  151 us
    pallas_call x1, Pallas kernels, gather_all(): pl.pallas_call(gather_kernel, in_specs=[ANY] * 3, out_specs=[ANY] * 3, ou...  81.4 us
    pallas_call x1, Pallas kernels, spmm_t(): pl.pallas_call(bwd_kernel, grid_spec=pltpu.PrefetchScalarGridSpec(num_sca...  45.3 us
    reduce_scatter x1, waiting for transfers between devices, local(): lax.psum_scatter(terms.astype(BF16), 'rep', scatter_dimension=0, tiled=True)  37.1 us
    pallas_call x1, Pallas kernels, spmm(): pl.pallas_call(fwd_kernel, grid_spec=pltpu.PrefetchScalarGridSpec(num_sca...  20.1 us
    all_to_all x1, blocking collectives, local(): activations = lax.all_to_all(act, 'rep', 1, 0, tiled=True)  13.6 us
    unnamed x4, waiting for transfers between devices  8.85 us
  transfers between devices with their start and end apart: 5, of which 4 were waited for; matrix products, arithmetic and copies ran while one was open for 4% of the time, Pallas kernels for 11%

profile of v2, /device:TPU:1, one launch (start us, length us, event | category | flops | bytes accessed | tf_op | source)
XLA Modules:
  0.0 415.6 jit_solution(11574395410272440740)
XLA Ops:
  7.2 1.4 copy.23.cols
  8.5 81.4 %gather_all.1 = (bf16[16,4096,128]{2,1,0:T(8,128)(2,1)}, bf16[8,512,128]{2,1,0:T(8,128)(2,1)}, bf16[8,1024,128]{2,1,0:T(8,128)(2,1)}) custom-call(bf16[4096,128]{1,0:T(8,128)(2,1)} %feats.1, bf16[4096,128]{1,0:T(8,128)(2,1)} %cot.1, bf16[1024,128]{1,0:T(8,128)(2,1)} %weight.1), custom_call_target="tpu_custom_call" | custom-call | tf_op jit(solution)/shard_map/gather_all/pallas_call | solution.py:202
  89.9 20.1 %spmm.1 = bf16[4096,128]{1,0:T(8,128)(2,1)} custom-call(s32[32,16]{1,0:T(8,128)} %copy.23.cols, s32[32]{0:T(128)} %counts.3, bf16[32,16,128,128]{3,2,1,0:T(8,128)(2,1)} %tiles.3, bf16[512,128,128]{2,1,0:T(8,128)(2,1)} %bitcast.36), custom_call_target="tpu_custom_call" | custom-call | tf_op jit(solution)/shard_map/spmm/pallas_call | solution.py:285
  110.1 0.0 copy-start.2
  110.1 2.4 copy.24
  112.5 4.2 %all-to-all-start = ((bf16[8,512,128]{1,2,0:T(8,128)(2,1)}), bf16[8,512,128]{1,2,0:T(8,128)(2,1)}, u32[]{:S(2)}, u32[]{:S(2)}) async-start(bf16[8,512,128]{1,2,0:T(8,128)(2,1)} %copy.24), calls=%async_computation | async-start | bytes 2097152 | tf_op jit(solution)/shard_map/all_to_all | solution.py:414
  116.8 0.0 reduce-scatter.8.cloned.1.call-start
  116.8 0.0 copy-done.2
  116.8 0.0 copy-start.3
  116.8 2.6 copy.25
  119.4 0.0 copy-done.3
  119.4 0.1 convert_bitcast_fusion
  119.6 1.8 copy.27
  121.4 0.0 copy-start.1
  121.4 3.1 copy.28
  124.5 7.2 %all-to-all-done = bf16[8,512,128]{1,2,0:T(8,128)(2,1)} async-done(((bf16[8,512,128]{1,2,0:T(8,128)(2,1)}), bf16[8,512,128]{1,2,0:T(8,128)(2,1)}, u32[]{:S(2)}, u32[]{:S(2)}) %all-to-all-start) | async-done | bytes 1048608 | tf_op jit(solution)/shard_map/all_to_all | solution.py:414
  131.7 0.0 copy-done.1
  131.7 3.9 multiply_convert_fusion
  135.7 0.0 copy-start.4
  135.7 1.0 copy-done.4
  136.6 3.8 convolution_convert_fusion
  140.5 0.0 reduce-scatter.8.cloned.1.call-update
  140.5 2.5 fusion
  143.0 1.2 copy.38
  144.1 3.6 all-to-all-start.2
  147.8 0.0 reduce-scatter.10.cloned.1.call-start
  147.8 37.1 %reduce-scatter.8.cloned.1.call-done = bf16[128,1024]{1,0:T(8,128)(2,1)} async-done(((bf16[1024,1024]{1,0:T(8,128)(2,1)}), bf16[128,1024]{1,0:T(8,128)(2,1)}) %reduce-scatter.8.cloned.1.call-update) | async-done | bytes 262160 | tf_op jit(solution)/shard_map/reduce_scatter | solution.py:425
  184.9 1.8 copy.32
  186.7 0.0 reduce-scatter.10.cloned.1.call-update
  186.7 0.0 reduce-scatter.6.cloned.1.call-start
  186.8 0.0 all-to-all-done.2
  186.8 0.0 copy-start
  186.8 1.0 copy-done
  187.8 45.3 %spmm_t.1 = bf16[512,128,128]{2,1,0:T(8,128)(2,1)} custom-call(s32[32,16]{1,0:T(8,128)} %copy.23.cols, s32[32]{0:T(128)} %counts.3, bf16[32,16,128,128]{3,2,1,0:T(8,128)(2,1)} %tiles.3, bf16[4096,128]{1,0:T(8,128)(2,1)} %bitcast.38), custom_call_target="tpu_custom_call" | custom-call | tf_op jit(solution)/shard_map/spmm_t/pallas_call | solution.py:382
  233.1 0.0 reduce-scatter.6.cloned.1.call-update
  233.1 0.2 copy.39
  233.3 13.6 %all_to_all.57 = bf16[512,8,128]{2,0,1:T(8,128)(2,1)S(1)} all-to-all(bf16[512,8,128]{2,0,1:T(8,128)(2,1)S(1)} %bitcast.41), channel_id=1, replica_groups=mesh['row'=16,'rep'=8] {'rep'}, dimensions={1} | all-to-all | bytes 2097152 | tf_op jit(solution)/shard_map/all_to_all | solution.py:418
  246.9 8.8 %reduce-scatter.10.cloned.1.call-done = bf16[64,128]{1,0:T(8,128)(2,1)} async-done(((bf16[1024,128]{1,0:T(8,128)(2,1)}), bf16[64,128]{1,0:T(8,128)(2,1)}) %reduce-scatter.10.cloned.1.call-update) | async-done | bytes 16400
  255.7 0.8 copy.33
  256.5 0.7 copy.31
  257.3 150.9 %reduce-scatter.6.cloned.1.call-done = bf16[4096,128]{1,0:T(8,128)(2,1)} async-done(((bf16[65536,128]{1,0:T(8,128)(2,1)}), bf16[4096,128]{1,0:T(8,128)(2,1)}) %reduce-scatter.6.cloned.1.call-update) | async-done | bytes 1048592 | tf_op jit(solution)/shard_map/reduce_scatter | solution.py:428
  408.1 1.0 copy.41
Async XLA Ops:
  110.1 6.7 %copy-start.2 = (bf16[8,1024,128]{2,1,0:T(8,128)(2,1)S(1)}, bf16[8,1024,128]{2,1,0:T(8,128)(2,1)}, u32[]{:S(2)}) copy-start(bf16[8,1024,128]{2,1,0:T(8,128)(2,1)} %get-tuple-element.7) | copy-start | bytes 6291460
  112.5 19.2 %all-to-all-start = ((bf16[8,512,128]{1,2,0:T(8,128)(2,1)}), bf16[8,512,128]{1,2,0:T(8,128)(2,1)}, u32[]{:S(2)}, u32[]{:S(2)}) async-start(bf16[8,512,128]{1,2,0:T(8,128)(2,1)} %copy.24), calls=%async_computation | async-start | bytes 2097152 | tf_op jit(solution)/shard_map/all_to_all | solution.py:414
  116.8 68.2 %reduce-scatter.8.cloned.1.call-start = ((), (), s32[]{:S(2)}) async-start(), calls=%async_computation.7 | async-start | bytes 2359296 | tf_op jit(solution)/shard_map/reduce_scatter | solution.py:425
  116.8 2.6 copy-start.3
  121.4 10.3 %copy-start.1 = (bf16[1024,8,128]{0,2,1:T(8,128)(2,1)S(1)}, bf16[1024,8,128]{0,2,1:T(8,128)(2,1)}, u32[]{:S(2)}) copy-start(bf16[1024,8,128]{0,2,1:T(8,128)(2,1)} %copy.25) | copy-start | bytes 6291460
  135.7 1.0 copy-start.4
  144.1 42.7 %all-to-all-start.2 = ((bf16[512,8,128]{2,0,1:T(8,128)(2,1)}), bf16[512,8,128]{2,0,1:T(8,128)(2,1)S(1)}, u32[]{:S(2)}, u32[]{:S(2)}) async-start(bf16[512,8,128]{2,0,1:T(8,128)(2,1)} %bitcast.33), calls=%async_computation.2 | async-start | bytes 2097152 | tf_op jit(solution)/shard_map/all_to_all | solution.py:423
  147.8 108.0 %reduce-scatter.10.cloned.1.call-start = ((), (), s32[]{:S(2)}) async-start(), calls=%async_computation.8 | async-start | bytes 278528
  186.7 221.4 %reduce-scatter.6.cloned.1.call-start = ((), (), s32[]{:S(2)}) async-start(), calls=%async_computation.6 | async-start | bytes 17825792 | tf_op jit(solution)/shard_map/reduce_scatter | solution.py:428
  186.8 1.0 copy-start
Sparse Core Ops, SparseCore 0:
  140.6 44.2 reduce-scatter.7
  189.2 66.5 reduce-scatter.9
  260.6 147.4 reduce-scatter.5

commit v3 on v2

--- a/solution.py
+++ b/solution.py
@@ -224,6 +224,300 @@
     )(features, cotangent, weight)
 
 
+STRIP = 128
+
+
+def dense_kernel(
+    mixed, cots, ws, mixed_grad, act, wgrad, m, w, cot, grad, back,
+    send_sems, m_recv, back_recv, local_sems,
+):
+    here = Place()
+    piece, width = mixed.shape[1:]
+    peers = [here.peer(d) for d in range(1, N_REP)]
+    first = pltpu.make_async_copy(mixed.at[here.rep], m.at[here.rep], local_sems.at[0])
+    first.start()
+    loads = []
+    for r in range(N_REP):
+        at = pl.ds(r * width, width)
+        loads.append(pltpu.make_async_copy(ws.at[r], w.at[:, at], local_sems.at[1 + r]))
+        loads.append(pltpu.make_async_copy(cots.at[r], cot.at[:, at], local_sems.at[9 + r]))
+    greet([(here.row, q) for q in peers])
+    send = Sends(send_sems)
+    for d, q in enumerate(peers):
+        send(mixed.at[q], m.at[here.rep], m_recv.at[d], (here.row, q))
+    for load in loads:
+        load.start()
+    for load in loads:
+        load.wait()
+    first.wait()
+    for d, q in enumerate(peers):
+        arrived(m.at[q], m_recv.at[d])
+
+    for i in range(piece // STRIP):
+        rows = pl.ds(i * STRIP, STRIP)
+        x = jnp.concatenate([m[r, rows, :] for r in range(N_REP)], axis=1)
+        pre = jnp.dot(x, w[...], preferred_element_type=F32)
+        sig = jax.nn.sigmoid(pre)
+        out = (pre * sig).astype(BF16)
+        g = (cot[rows, :].astype(F32) * sig * (1.0 + pre * (1.0 - sig))).astype(BF16)
+        grad[rows, :] = g
+        b = lax.dot_general(
+            g, w[...], (((1,), (1,)), ((), ())), preferred_element_type=F32
+        ).astype(BF16)
+        for r in range(N_REP):
+            act[r, rows, :] = out[:, r * width : (r + 1) * width]
+            back[r, rows, :] = b[:, r * width : (r + 1) * width]
+        for d, q in enumerate(peers):
+            send(
+                back.at[q, rows], mixed_grad.at[here.rep, rows], back_recv.at[d, i],
+                (here.row, q),
+            )
+    last = pltpu.make_async_copy(back.at[here.rep], mixed_grad.at[here.rep], local_sems.at[0])
+    last.start()
+    for r in range(N_REP):
+        wgrad[r] = lax.dot_general(
+            m[r], grad[...], (((0,), (0,)), ((), ())), preferred_element_type=F32
+        ).astype(BF16)
+    last.wait()
+    for d, q in enumerate(peers):
+        for i in range(piece // STRIP):
+            arrived(mixed_grad.at[q, pl.ds(i * STRIP, STRIP)], back_recv.at[d, i])
+    send.finish()
+
+
+def dense(mixed, cots, ws):
+    n, piece, width = mixed.shape
+    strips = piece // STRIP
+    return pl.pallas_call(
+        dense_kernel,
+        in_specs=[ANY] * 3,
+        out_specs=[ANY, VM, VM],
+        out_shape=[
+            jax.ShapeDtypeStruct(mixed.shape, BF16),
+            jax.ShapeDtypeStruct(mixed.shape, BF16),
+            jax.ShapeDtypeStruct((n, width, n * width), BF16),
+        ],
+        scratch_shapes=[
+            pltpu.VMEM((n, piece, width), BF16),
+            pltpu.VMEM((n * width, n * width), BF16),
+            pltpu.VMEM((piece, n * width), BF16),
+            pltpu.VMEM((piece, n * width), BF16),
+            pltpu.VMEM((n, piece, width), BF16),
+            pltpu.SemaphoreType.DMA(((n - 1) * (1 + strips),)),
+            pltpu.SemaphoreType.DMA((n - 1,)),
+            pltpu.SemaphoreType.DMA((n - 1, strips)),
+            pltpu.SemaphoreType.DMA((17,)),
+        ],
+        compiler_params=pltpu.CompilerParams(collective_id=1, has_side_effects=True),
+        name="dense",
+    )(mixed, cots, ws)
+
+
+OFFSETS = (2, 1, -1, 0)
+SUM_ROWS = 128
+
+
+def reduce_kernel(
+    part, act, wgrad, act_out, out, wg_out,
+    own, theirs, far_up, far_down, near_up, near_down, cross, own_act,
+    wg_in, wg_sum, wg_sib, wg_half, wg_row, wg_fin, wg_fin_sib,
+    send_sems, load_sems, sib_recv, far_recv, near_recv, cross_recv,
+    act_recv, wg_recv, row_recv, pair_recv, local_sems,
+):
+    here = Place()
+    step = own.shape[1] // CHUNKS
+    half = CHUNKS // 2
+    peers = [here.peer(d) for d in range(1, N_REP)]
+    sib = here.at(False, 0, True)
+    up, down, across = here.at(False, 1), here.at(False, -1), here.at(True, 0)
+    columns = [(o, dy) for o in (True, False) for dy in OFFSETS][:-1]
+
+    def rows(i):
+        return pl.ds(i * step, step)
+
+    loads = {}
+    for r in range(8):
+        slot = here.slot(r < 4, OFFSETS[r % 4])
+        for i in range(CHUNKS):
+            loads[r, i] = pltpu.make_async_copy(
+                part.at[slot, rows(i)], own.at[r, rows(i)], load_sems.at[r, i]
+            )
+    extra = [
+        pltpu.make_async_copy(act.at[here.rep], own_act, local_sems.at[0]),
+        pltpu.make_async_copy(wgrad.at[here.rep], wg_in.at[N_REP - 1], local_sems.at[1]),
+    ]
+    for load in extra:
+        load.start()
+    for load in loads.values():
+        load.start()
+    greet([sib] + [here.at(*column) for column in columns] + [(here.row, q) for q in peers])
+
+    send = Sends(send_sems)
+    order = [0, 4, 1, 2, 3, 5, 6, 7]
+    for r in order:
+        slot = here.slot(r < 4, OFFSETS[r % 4], True)
+        for i in range(CHUNKS):
+            send(part.at[slot, rows(i)], theirs.at[r, rows(i)], sib_recv.at[r, i], sib)
+
+    def total(r, i, more, dst=None):
+        loads[r, i].wait()
+        arrived(theirs.at[r, rows(i)], sib_recv.at[r, i])
+        target = own.at[r] if dst is None else dst
+
+        @pl.loop(0, step // SUM_ROWS)
+        def _(j):
+            at = pl.ds(pl.multiple_of(i * step + j * SUM_ROWS, SUM_ROWS), SUM_ROWS)
+            acc = own[r, at, :].astype(F32) + theirs[r, at, :].astype(F32)
+            for ref, base in more:
+                at2 = pl.ds(pl.multiple_of(base * step + j * SUM_ROWS, SUM_ROWS), SUM_ROWS)
+                acc = acc + ref[at2, :].astype(F32)
+            target[at, :] = acc.astype(BF16)
+
+    def far(hh):
+        for i in range(half):
+            total(4 * hh, i, [])
+            send(own.at[4 * hh, rows(i)], far_up.at[hh, rows(i)], far_recv.at[hh, 0, i], up)
+            total(4 * hh, i + half, [])
+            send(
+                own.at[4 * hh, rows(i + half)], far_down.at[hh, rows(i)],
+                far_recv.at[hh, 1, i], down,
+            )
+
+    def near(hh, i, j, up_more, down_more):
+        r, s = 4 * hh + 1, 4 * hh + 2
+        total(r, i, up_more)
+        send(own.at[r, rows(i)], near_up.at[hh, rows(i)], near_recv.at[hh, 0, i], up)
+        total(s, j, down_more)
+        send(own.at[s, rows(j)], near_down.at[hh, rows(j)], near_recv.at[hh, 1, j], down)
+
+    def near_first(hh):
+        for i in range(half):
+            near(hh, i + half, i, [], [])
+
+    def near_last(hh):
+        for i in range(half):
+            arrived(far_up.at[hh, rows(i)], far_recv.at[hh, 0, i])
+            arrived(far_down.at[hh, rows(i)], far_recv.at[hh, 1, i])
+            near(hh, i, i + half, [(far_up.at[hh], i)], [(far_down.at[hh], i)])
+
+    def final(hh):
+        for i in (0, 2, 1, 3):
+            arrived(near_up.at[hh, rows(i)], near_recv.at[hh, 0, i])
+            arrived(near_down.at[hh, rows(i)], near_recv.at[hh, 1, i])
+            more = [(near_up.at[hh], i), (near_down.at[hh], i)]
+            if hh == 0:
+                total(3, i, more)
+                send(own.at[3, rows(i)], cross.at[rows(i)], cross_recv.at[i], across)
+            else:
+                arrived(cross.at[rows(i)], cross_recv.at[i])
+                total(7, i, more + [(cross, i)], out)
+
+    far(0)
+    for d, q in enumerate(peers):
+        send(wgrad.at[q], wg_in.at[d], wg_recv.at[d], (here.row, q))
+    for d, q in enumerate(peers):
+        send(act.at[q], act_out.at[here.rep], act_recv.at[d], (here.row, q))
+    extra[0].wait()
+    keep = pltpu.make_async_copy(own_act, act_out.at[here.rep], local_sems.at[0])
+    keep.start()
+    near_first(0)
+    far(1)
+    near_last(0)
+    near_first(1)
+    final(0)
+
+    extra[1].wait()
+    for d in range(N_REP - 1):
+        arrived(wg_in.at[d], wg_recv.at[d])
+    wide = wg_in.shape[2]
+    edge = wg_half.shape[1]
+
+    @pl.loop(0, wide // 128)
+    def _(j):
+        at = pl.ds(pl.multiple_of(j * 128, 128), 128)
+        acc = wg_in[0, :, at].astype(F32)
+        for d in range(1, N_REP):
+            acc = acc + wg_in[d, :, at].astype(F32)
+        acc = acc.astype(BF16)
+        wg_sum[0, j] = acc[:edge]
+        wg_sum[1, j] = acc[edge:]
+
+    send(wg_sum.at[1 - here.c], wg_sib, pair_recv.at[0], sib)
+    near_last(1)
+    arrived(wg_sib, pair_recv.at[0])
+
+    @pl.loop(0, wide // 128)
+    def _(j):
+        wg_half[j] = (wg_sum[here.c, j].astype(F32) + wg_sib[j].astype(F32)).astype(BF16)
+
+    for k, (o, dy) in enumerate(columns):
+        send(
+            wg_half.at[here.slot(o, dy) // 2], wg_row.at[k], row_recv.at[k], here.at(o, dy)
+        )
+    for k in range(len(columns)):
+        arrived(wg_row.at[k], row_recv.at[k])
+    acc = wg_half[here.row // 2].astype(F32)
+    for k in range(len(columns)):
+        acc = acc + wg_row[k].astype(F32)
+    wg_fin[...] = acc
+    send(wg_fin, wg_fin_sib, pair_recv.at[1], sib)
+    final(1)
+    arrived(wg_fin_sib, pair_recv.at[1])
+
+    @pl.when(here.c == 0)
+    def _():
+        wg_out[:edge, :] = wg_fin[:, :edge]
+        wg_out[edge:, :] = wg_fin_sib[:, :edge]
+
+    @pl.when(here.c == 1)
+    def _():
+        wg_out[:edge, :] = wg_fin_sib[:, edge:]
+        wg_out[edge:, :] = wg_fin[:, edge:]
+
+    keep.wait()
+    for d, q in enumerate(peers):
+        arrived(act_out.at[q], act_recv.at[d])
+    send.finish()
+
+
+def reduce_all(part, act, wgrad):
+    n, rows, width = part.shape
+    n_rep, k, wide = wgrad.shape
+    edge = k // 2
+    dma = pltpu.SemaphoreType.DMA
+    return pl.pallas_call(
+        reduce_kernel,
+        in_specs=[ANY] * 3,
+        out_specs=[ANY, VM, VM],
+        out_shape=[
+            jax.ShapeDtypeStruct(act.shape, BF16),
+            jax.ShapeDtypeStruct((rows, width), BF16),
+            jax.ShapeDtypeStruct((k, wide // n), F32),
+        ],
+        scratch_shapes=[
+            pltpu.VMEM((8, rows, width), BF16),
+            pltpu.VMEM((8, rows, width), BF16),
+            pltpu.VMEM((2, rows // 2, width), BF16),
+            pltpu.VMEM((2, rows // 2, width), BF16),
+            pltpu.VMEM((2, rows, width), BF16),
+            pltpu.VMEM((2, rows, width), BF16),
+            pltpu.VMEM((rows, width), BF16),
+            pltpu.VMEM(act.shape[1:], BF16),
+            pltpu.VMEM(wgrad.shape, BF16),
+            pltpu.VMEM((2, wide // 128, edge, 128), BF16),
+            pltpu.VMEM((wide // 128, edge, 128), BF16),
+            pltpu.VMEM((wide // 128, edge, 128), BF16),
+            pltpu.VMEM((7, edge, 128), BF16),
+            pltpu.VMEM((edge, 128), F32),
+            pltpu.VMEM((edge, 128), F32),
+            dma((83,)), dma((8, CHUNKS)), dma((8, CHUNKS)), dma((2, 2, 2)), dma((2, 2, CHUNKS)),
+            dma((CHUNKS,)), dma((7,)), dma((7,)), dma((7,)), dma((2,)), dma((2,)),
+        ],
+        compiler_params=pltpu.CompilerParams(collective_id=2, has_side_effects=True),
+        name="reduce_all",
+    )(part, act, wgrad)
+
+
 SLOTS_AHEAD = 4
 
 
@@ -407,28 +701,14 @@
     rows_here, feat_local = features.shape
     blocks_here, slots, t, _ = tiles.shape
     total_blocks = blocks_here * lax.axis_size("row")
-    gathered, cot, w = gather_all(features, cotangent, weight)
-    cot = jnp.swapaxes(cot, 0, 1).reshape(-1, N_REP * feat_local)
-    w = jnp.swapaxes(w, 0, 1).reshape(-1, N_REP * feat_local)
+    gathered, cots, ws = gather_all(features, cotangent, weight)
     mixed = spmm(gathered.reshape(total_blocks, t, feat_local), tiles, columns, counts)
-    mixed = lax.all_to_all(mixed, "rep", 0, 1, tiled=True)
-    preact = jnp.dot(mixed, w, preferred_element_type=F32)
-    sig = jax.nn.sigmoid(preact)
-    act = (preact * sig).astype(BF16)
-    activations = lax.all_to_all(act, "rep", 1, 0, tiled=True)
-    grad_out = (cot.astype(F32) * sig * (1.0 + preact * (1.0 - sig))).astype(BF16)
-    mixed_grad = lax.dot_general(
-        grad_out, w, (((1,), (1,)), ((), ())), preferred_element_type=F32
-    ).astype(BF16)
-    mixed_grad = lax.all_to_all(mixed_grad, "rep", 1, 0, tiled=True)
-    terms = lax.dot_general(mixed, grad_out, (((0,), (0,)), ((), ())), preferred_element_type=F32)
-    terms = lax.psum_scatter(terms.astype(BF16), "rep", scatter_dimension=0, tiled=True)
-    weight_grad = lax.psum_scatter(terms, "row", scatter_dimension=1, tiled=True).astype(F32)
-    partial = spmm_t(mixed_grad, tiles, columns, counts, total_blocks)
-    feature_grad = lax.psum_scatter(
-        partial.reshape(total_blocks * t, feat_local), "row", scatter_dimension=0, tiled=True
+    mixed_grad, act, wgrad = dense(mixed.reshape(N_REP, -1, feat_local), cots, ws)
+    part = spmm_t(mixed_grad.reshape(mixed.shape), tiles, columns, counts, total_blocks)
+    act, feature_grad, weight_grad = reduce_all(
+        part.reshape(N_ROW, rows_here, feat_local), act, wgrad
     )
-    return activations, feature_grad, weight_grad
+    return act.reshape(features.shape), feature_grad, weight_grad
 
 
 def solution(mesh):

time: 417 us -> 273 us (0.65)
  waiting for transfers between devices: 204 us -> 0 us
  Pallas kernels: 147 us -> 267 us
  blocking collectives: 13.6 us -> 0 us
  between operations: 13.9 us -> 0.67 us
  local copies, waits for them, and re-layouts: 18.9 us -> 7.44 us
  matrix products: 10.2 us -> 0 us
  starting transfers between devices: 7.99 us -> 0 us
    reduce_scatter x2 -> x0, waiting for transfers between devices: 188 us -> none  [the longest x1 151 us: local(): lax.psum_scatter(partial.reshape(total_blocks * t, feat_local), 'row', sc...]
    pallas_call x0 -> x2, Pallas kernels: none -> 125 us  [the longest x1 95.5 us: reduce_all(): pl.pallas_call(reduce_kernel, in_specs=[ANY] * 3, out_specs=[ANY, VM, VM]...]
    all_to_all x1 -> x0, blocking collectives: 13.6 us -> none  [local(): activations = lax.all_to_all(act, 'rep', 1, 0, tiled=True)]
    dot_general x3 -> x0, matrix products: 10.2 us -> none  [the longest x1 3.93 us: local(): preact = jnp.dot(mixed, w, preferred_element_type=F32)]
    unnamed x4 -> x0, waiting for transfers between devices: 8.85 us -> none
    all_to_all x2 -> x0, starting transfers between devices: 7.87 us -> none  [the longest x1 4.24 us: local(): mixed = lax.all_to_all(mixed, 'rep', 0, 1, tiled=True)]
    all_to_all x2 -> x0, waiting for transfers between devices: 7.23 us -> none  [the longest x1 7.23 us: local(): mixed = lax.all_to_all(mixed, 'rep', 0, 1, tiled=True)]
    convert_element_type x2 -> x0, local copies, waits for them, and re-layouts: 4.9 us -> none  [local(): cot.astype(F32) * sig * (1.0 + preact * (1.0 - sig))]
  transfers between devices with their start and end apart: 5 -> 0, of which waited for: 4 -> 0; matrix products, arithmetic and copies ran while one was open for 4% -> 0% of each run, Pallas kernels for 11% -> 0%
where the time goes in v3:
time: 273 us; the launch traced here: 276 us
  Pallas kernels  267 us (98%)
  local copies, waits for them, and re-layouts  7.44 us (3%)
    pallas_call x1, Pallas kernels, reduce_all(): pl.pallas_call(reduce_kernel, in_specs=[ANY] * 3, out_specs=[ANY, VM, VM]...  95.5 us
    pallas_call x1, Pallas kernels, gather_all(): pl.pallas_call(gather_kernel, in_specs=[ANY] * 3, out_specs=[ANY] * 3, ou...  81.4 us
    pallas_call x1, Pallas kernels, spmm_t(): pl.pallas_call(bwd_kernel, grid_spec=pltpu.PrefetchScalarGridSpec(num_sca...  42.4 us
    pallas_call x1, Pallas kernels, dense(): pl.pallas_call(dense_kernel, in_specs=[ANY] * 3, out_specs=[ANY, VM, VM],...  29.3 us
    pallas_call x1, Pallas kernels, spmm(): pl.pallas_call(fwd_kernel, grid_spec=pltpu.PrefetchScalarGridSpec(num_sca...  18.8 us
    unnamed x4, local copies, waits for them, and re-layouts  7.44 us

profile of v3, /device:TPU:1, one launch (start us, length us, event | category | flops | bytes accessed | tf_op | source)
XLA Modules:
  0.0 275.5 jit_solution(5369372676261327736)
XLA Ops:
  0.6 1.4 copy.10.cols
  2.0 81.4 %gather_all.1 = (bf16[16,4096,128]{2,1,0:T(8,128)(2,1)}, bf16[8,512,128]{2,1,0:T(8,128)(2,1)}, bf16[8,1024,128]{2,1,0:T(8,128)(2,1)}) custom-call(bf16[4096,128]{1,0:T(8,128)(2,1)} %feats.1, bf16[4096,128]{1,0:T(8,128)(2,1)} %cot.1, bf16[1024,128]{1,0:T(8,128)(2,1)} %weight.1), custom_call_target="tpu_custom_call" | custom-call | tf_op jit(solution)/shard_map/gather_all/pallas_call | solution.py:202
  83.4 18.8 %spmm.1 = bf16[4096,128]{1,0:T(8,128)(2,1)} custom-call(s32[32,16]{1,0:T(8,128)} %copy.10.cols, s32[32]{0:T(128)} %counts.3, bf16[32,16,128,128]{3,2,1,0:T(8,128)(2,1)} %tiles.3, bf16[512,128,128]{2,1,0:T(8,128)(2,1)} %bitcast.6), custom_call_target="tpu_custom_call" | custom-call | tf_op jit(solution)/shard_map/spmm/pallas_call | solution.py:579
  102.2 29.3 %dense.1 = (bf16[8,512,128]{2,1,0:T(8,128)(2,1)}, bf16[8,512,128]{2,1,0:T(8,128)(2,1)}, bf16[8,128,1024]{2,1,0:T(8,128)(2,1)}) custom-call(bf16[8,512,128]{2,1,0:T(8,128)(2,1)} %bitcast.7, bf16[8,512,128]{2,1,0:T(8,128)(2,1)} %get-tuple-element.13.cots, bf16[8,1024,128]{2,1,0:T(8,128)(2,1)} %get-tuple-element.14.ws), custom_call_target="tpu_custom_call" | custom-call | tf_op jit(solution)/shard_map/dense/pallas_call | solution.py:291
  131.5 42.4 %spmm_t.1 = bf16[512,128,128]{2,1,0:T(8,128)(2,1)} custom-call(s32[32,16]{1,0:T(8,128)} %copy.10.cols, s32[32]{0:T(128)} %counts.3, bf16[32,16,128,128]{3,2,1,0:T(8,128)(2,1)} %tiles.3, bf16[4096,128]{1,0:T(8,128)(2,1)} %bitcast.8), custom_call_target="tpu_custom_call" | custom-call | tf_op jit(solution)/shard_map/spmm_t/pallas_call | solution.py:676
  173.9 95.5 %reduce_all.1 = (bf16[8,512,128]{2,1,0:T(8,128)(2,1)}, bf16[4096,128]{1,0:T(8,128)(2,1)}, f32[128,64]{1,0:T(8,128)}) custom-call(bf16[16,4096,128]{2,1,0:T(8,128)(2,1)} %bitcast.5, bf16[8,512,128]{2,1,0:T(8,128)(2,1)} %get-tuple-element.16.act, bf16[8,128,1024]{2,1,0:T(8,128)(2,1)} %get-tuple-element.17.wgrad), custom_call_target="tpu_custom_call" | custom-call | tf_op jit(solution)/shard_map/reduce_all/pallas_call | solution.py:488
  269.5 1.5 copy.11
  271.0 2.3 copy.14
  273.3 2.3 copy.15

commit v4 on v3

--- a/solution.py
+++ b/solution.py
@@ -78,7 +78,7 @@
     pltpu.make_async_copy(dst, dst, recv_sem).wait()
 
 
-CHUNKS = 4
+CHUNKS = 8
 
 
 def gather_kernel(
@@ -401,7 +401,7 @@
             near(hh, i, i + half, [(far_up.at[hh], i)], [(far_down.at[hh], i)])
 
     def final(hh):
-        for i in (0, 2, 1, 3):
+        for i in [k + part for k in range(half) for part in (0, half)]:
             arrived(near_up.at[hh, rows(i)], near_recv.at[hh, 0, i])
             arrived(near_down.at[hh, rows(i)], near_recv.at[hh, 1, i])
             more = [(near_up.at[hh], i), (near_down.at[hh], i)]
@@ -510,7 +510,7 @@
             pltpu.VMEM((7, edge, 128), BF16),
             pltpu.VMEM((edge, 128), F32),
             pltpu.VMEM((edge, 128), F32),
-            dma((83,)), dma((8, CHUNKS)), dma((8, CHUNKS)), dma((2, 2, 2)), dma((2, 2, CHUNKS)),
+            dma((15 * CHUNKS + 23,)), dma((8, CHUNKS)), dma((8, CHUNKS)), dma((2, 2, CHUNKS // 2)), dma((2, 2, CHUNKS)),
             dma((CHUNKS,)), dma((7,)), dma((7,)), dma((7,)), dma((2,)), dma((2,)),
         ],
         compiler_params=pltpu.CompilerParams(collective_id=2, has_side_effects=True),
@@ -529,7 +529,7 @@
         at = pl.ds(pl.multiple_of(k * t, t), t)
         return (
             pltpu.make_async_copy(tiles.at[b, k], tbuf.at[s, :, at], sems.at[s, k, 0]),
-            pltpu.make_async_copy(gathered.at[cols[b, k]], gbuf.at[s, at, :], sems.at[s, k, 1]),
+            pltpu.make_async_copy(gathered.at[cols[k, b]], gbuf.at[s, at, :], sems.at[s, k, 1]),
         )
 
     def start(b):
@@ -601,22 +601,27 @@
 def bwd_kernel(cols, counts, tiles, grad, out, acc, tbuf, stage, sems, out_sems):
     blocks, slots, t, _ = tiles.shape
     total = acc.shape[0]
-
-    def copy(b, k):
+    groups = slots // GROUP
+
+    def copy(b, q):
         s = lax.rem(b, SLOTS_AHEAD)
-        return pltpu.make_async_copy(tiles.at[b, k], tbuf.at[s, k], sems.at[s, k])
+        at = pl.ds(q * GROUP, GROUP)
+        return pltpu.make_async_copy(tiles.at[b, at], tbuf.at[s, at], sems.at[s, q])
 
     def start(b):
-        @pl.loop(0, counts[b])
-        def _(k):
-            copy(b, k).start()
+        for q in range(groups):
+
+            @pl.when(q * GROUP < counts[b])
+            def _():
+                copy(b, q).start()
 
     for b in range(SLOTS_AHEAD - 1):
         start(b)
 
-    @pl.loop(0, total)
+    @pl.loop(0, total // 4)
     def _(j):
-        acc[j] = jnp.zeros(acc.shape[1:], F32)
+        for i in range(4):
+            acc[4 * j + i] = jnp.zeros(acc.shape[1:], F32)
 
     @pl.loop(0, blocks)
     def _(b):
@@ -627,24 +632,26 @@
             start(b + SLOTS_AHEAD - 1)
 
         n = counts[b]
-
-        @pl.loop(0, n)
-        def _(k):
-            copy(b, k).wait()
-
-        g = grad[pl.ds(pl.multiple_of(b * t, t), t), :]
-
-        @pl.loop(0, (n + GROUP - 1) // GROUP)
-        def _(q):
-            terms = []
-            for i in range(GROUP):
-                k = q * GROUP + i
-                term = lax.dot_general(
-                    tbuf[s, k], g, (((0,), (0,)), ((), ())), preferred_element_type=F32
-                )
-                terms.append(jnp.where(k < n, term, 0.0))
-            for i in range(GROUP):
-                acc[cols[b, q * GROUP + i]] += terms[i]
+        for live in range(1, groups + 1):
+
+            @pl.when((n + GROUP - 1) // GROUP == live)
+            def _():
+                g = grad[pl.ds(pl.multiple_of(b * t, t), t), :]
+                for q in range(live):
+                    copy(b, q).wait()
+                for q in range(live):
+                    wide = jnp.concatenate(
+                        [tbuf[s, q * GROUP + i] for i in range(GROUP)], axis=1
+                    )
+                    terms = lax.dot_general(
+                        wide, g, (((0,), (0,)), ((), ())), preferred_element_type=F32
+                    )
+                    for i in range(GROUP):
+                        k = q * GROUP + i
+                        term = terms[i * t : (i + 1) * t]
+                        if q == live - 1 and i > 0:
+                            term = jnp.where(k < n, term, 0.0)
+                        acc[cols[k, b]] += term
 
     def flush(c):
         s = lax.rem(c, 2)
@@ -660,9 +667,10 @@
         def _():
             flush(c - 2).wait()
 
-        @pl.loop(0, OUT_CHUNK)
+        @pl.loop(0, OUT_CHUNK // 4)
         def _(j):
-            stage[s, j] = acc[c * OUT_CHUNK + j].astype(BF16)
+            for i in range(4):
+                stage[s, 4 * j + i] = acc[c * OUT_CHUNK + 4 * j + i].astype(BF16)
 
         flush(c).start()
 
@@ -687,7 +695,7 @@
                 pltpu.VMEM((total, t, width), F32),
                 pltpu.VMEM((SLOTS_AHEAD, slots, t, t), BF16),
                 pltpu.VMEM((2, OUT_CHUNK, t, width), BF16),
-                pltpu.SemaphoreType.DMA((SLOTS_AHEAD, slots)),
+                pltpu.SemaphoreType.DMA((SLOTS_AHEAD, slots // GROUP)),
                 pltpu.SemaphoreType.DMA((2,)),
             ],
         ),
@@ -701,6 +709,7 @@
     rows_here, feat_local = features.shape
     blocks_here, slots, t, _ = tiles.shape
     total_blocks = blocks_here * lax.axis_size("row")
+    columns = columns.T
     gathered, cots, ws = gather_all(features, cotangent, weight)
     mixed = spmm(gathered.reshape(total_blocks, t, feat_local), tiles, columns, counts)
     mixed_grad, act, wgrad = dense(mixed.reshape(N_REP, -1, feat_local), cots, ws)

time: 273 us -> 257 us (0.941); the launches traced: 276 us -> 256 us
  Pallas kernels: 267 us -> 249 us
    pallas_call x1, Pallas kernels: 95.5 us -> 81 us  [reduce_all(): pl.pallas_call(reduce_kernel, in_specs=[ANY] * 3, out_specs=[ANY, VM, VM]...]
    pallas_call x1, Pallas kernels: 42.4 us -> 30 us  [spmm_t(): pl.pallas_call(bwd_kernel, grid_spec=pltpu.PrefetchScalarGridSpec(num_sca...]
    pallas_call x1, Pallas kernels: 29.3 us -> 36.5 us  [dense(): pl.pallas_call(dense_kernel, in_specs=[ANY] * 3, out_specs=[ANY, VM, VM],...]
    unnamed x4 -> x3, local copies, waits for them, and re-layouts: 7.44 us -> 6.06 us
where the time goes in v4:
time: 257 us; the launch traced here: 256 us
  Pallas kernels  249 us (97%)
  local copies, waits for them, and re-layouts  6.06 us (2%)
    pallas_call x1, Pallas kernels, gather_all(): pl.pallas_call(gather_kernel, in_specs=[ANY] * 3, out_specs=[ANY] * 3, ou...  82.6 us
    pallas_call x1, Pallas kernels, reduce_all(): pl.pallas_call(reduce_kernel, in_specs=[ANY] * 3, out_specs=[ANY, VM, VM]...  81 us
    pallas_call x1, Pallas kernels, dense(): pl.pallas_call(dense_kernel, in_specs=[ANY] * 3, out_specs=[ANY, VM, VM],...  36.5 us
    pallas_call x1, Pallas kernels, spmm_t(): pl.pallas_call(bwd_kernel, grid_spec=pltpu.PrefetchScalarGridSpec(num_sca...  30 us
    pallas_call x1, Pallas kernels, spmm(): pl.pallas_call(fwd_kernel, grid_spec=pltpu.PrefetchScalarGridSpec(num_sca...  18.9 us
    unnamed x3, local copies, waits for them, and re-layouts  6.06 us

profile of v4, /device:TPU:1, one launch (start us, length us, event | category | flops | bytes accessed | tf_op | source)
XLA Modules:
  0.0 255.8 jit_solution(9953222038008165733)
XLA Ops:
  0.6 82.6 %gather_all.1 = (bf16[16,4096,128]{2,1,0:T(8,128)(2,1)}, bf16[8,512,128]{2,1,0:T(8,128)(2,1)}, bf16[8,1024,128]{2,1,0:T(8,128)(2,1)}) custom-call(bf16[4096,128]{1,0:T(8,128)(2,1)} %feats.1, bf16[4096,128]{1,0:T(8,128)(2,1)} %cot.1, bf16[1024,128]{1,0:T(8,128)(2,1)} %weight.1), custom_call_target="tpu_custom_call" | custom-call | tf_op jit(solution)/shard_map/gather_all/pallas_call | solution.py:202
  83.2 18.9 %spmm.1 = bf16[4096,128]{1,0:T(8,128)(2,1)} custom-call(s32[16,32]{1,0:T(8,128)} %bitcast.11, s32[32]{0:T(128)} %counts.3, bf16[32,16,128,128]{3,2,1,0:T(8,128)(2,1)} %tiles.3, bf16[512,128,128]{2,1,0:T(8,128)(2,1)} %bitcast.7), custom_call_target="tpu_custom_call" | custom-call | tf_op jit(solution)/shard_map/spmm/pallas_call | solution.py:579
  102.2 36.5 %dense.1 = (bf16[8,512,128]{2,1,0:T(8,128)(2,1)}, bf16[8,512,128]{2,1,0:T(8,128)(2,1)}, bf16[8,128,1024]{2,1,0:T(8,128)(2,1)}) custom-call(bf16[8,512,128]{2,1,0:T(8,128)(2,1)} %bitcast.8, bf16[8,512,128]{2,1,0:T(8,128)(2,1)} %get-tuple-element.13.cots, bf16[8,1024,128]{2,1,0:T(8,128)(2,1)} %get-tuple-element.14.ws), custom_call_target="tpu_custom_call" | custom-call | tf_op jit(solution)/shard_map/dense/pallas_call | solution.py:291
  138.7 30.0 %spmm_t.1 = bf16[512,128,128]{2,1,0:T(8,128)(2,1)} custom-call(s32[16,32]{1,0:T(8,128)} %bitcast.12, s32[32]{0:T(128)} %counts.3, bf16[32,16,128,128]{3,2,1,0:T(8,128)(2,1)} %tiles.3, bf16[4096,128]{1,0:T(8,128)(2,1)} %bitcast.10), custom_call_target="tpu_custom_call" | custom-call | tf_op jit(solution)/shard_map/spmm_t/pallas_call | solution.py:684
  168.7 81.0 %reduce_all.1 = (bf16[8,512,128]{2,1,0:T(8,128)(2,1)}, bf16[4096,128]{1,0:T(8,128)(2,1)}, f32[128,64]{1,0:T(8,128)}) custom-call(bf16[16,4096,128]{2,1,0:T(8,128)(2,1)} %bitcast.6, bf16[8,512,128]{2,1,0:T(8,128)(2,1)} %get-tuple-element.16.act, bf16[8,128,1024]{2,1,0:T(8,128)(2,1)} %get-tuple-element.17.wgrad), custom_call_target="tpu_custom_call" | custom-call | tf_op jit(solution)/shard_map/reduce_all/pallas_call | solution.py:488
  249.7 1.5 copy.9
  251.2 2.3 copy.12
  253.5 2.3 copy.13

commit v5 on v4

--- a/solution.py
+++ b/solution.py
@@ -32,6 +32,12 @@
 
     def at(self, other, dy, sib=False):
         return (self.slot(other, dy, sib), self.rep)
+
+    def peer_at(self, d):
+        x = lax.rem(self.rep // 4 + d // 4, 2)
+        z1 = lax.rem(lax.rem(self.rep, 4) // 2 + lax.rem(d, 4) // 2, 2)
+        z0 = lax.rem(self.rep + d, 2)
+        return x * 4 + z1 * 2 + z0
 
     def peer(self, d):
         x, z = self.rep // 4, lax.rem(self.rep, 4)
@@ -78,201 +84,161 @@
     pltpu.make_async_copy(dst, dst, recv_sem).wait()
 
 
-CHUNKS = 8
-
-
-def gather_kernel(
-    feats, cot, weight, gathered, cots, ws, own, own_w, own_c,
-    send_sems, recv_sems, cot_recv, w_recv, w_sib, local_sems,
+CHUNKS = 4
+
+
+STRIP = 128
+PAIR = 2
+
+
+def forward_kernel(
+    feats, cot, weight, tiles, cols, counts, mixed_grad, act, wgrad,
+    full, blocks, cots, ws, w, mixed, m, grad, back,
+    send_sems, recv_sems, cot_recv, w_recv, w_sib, m_send, m_recv, back_recv, local_sems,
 ):
     here = Place()
-    step = feats.shape[0] // CHUNKS
+    n_blocks, slots, t, _ = tiles.shape
+    step = n_blocks // CHUNKS
     piece = cot.shape[0] // N_REP
+    width = cot.shape[1]
     half = weight.shape[0] // 2
     peers = [here.peer(d) for d in range(1, N_REP)]
     sib = here.at(False, 0, True)
     up, down, across = here.at(False, 1), here.at(False, -1), here.at(True, 0)
 
-    loads = [
-        pltpu.make_async_copy(feats, own, local_sems.at[0]),
-        pltpu.make_async_copy(weight, own_w, local_sems.at[1]),
+    def base(slot):
+        return slot * n_blocks
+
+    own = [
+        pltpu.make_async_copy(feats, full.at[pl.ds(base(here.row), n_blocks)], local_sems.at[0]),
+        pltpu.make_async_copy(weight, ws.at[here.rep], local_sems.at[1]),
         pltpu.make_async_copy(
-            cot.at[pl.ds(pl.multiple_of(here.rep * piece, piece), piece)], own_c, local_sems.at[2]
+            cot.at[pl.ds(pl.multiple_of(here.rep * piece, piece), piece)],
+            cots.at[here.rep], local_sems.at[2],
         ),
+        pltpu.make_async_copy(tiles, blocks, local_sems.at[3]),
     ]
-    for load in loads:
-        load.start()
     greet([sib, up, down, across] + [(here.row, q) for q in peers])
-
     send = Sends(send_sems)
 
     def rows(chunk):
         return pl.ds(chunk * step, step)
 
     def place(slot, chunk):
-        return gathered.at[slot, rows(chunk)]
-
-    slots = [
-        here.slot(False, -1), here.slot(False, 1), here.slot(False, 2), here.slot(True, 0),
-        here.slot(True, -1), here.slot(True, 1), here.slot(True, 2),
+        return full.at[pl.ds(base(slot) + chunk * step, step)]
+
+    columns = [
+        (False, -1), (False, 1), (False, 2), (True, 0), (True, -1), (True, 1), (True, 2),
     ]
-
-    def launch(src_of, slot, order, base, to_x, sib_kind):
-        for i in range(CHUNKS):
-            if to_x:
-                send(src_of(i), place(slot, i), recv_sems.at[3, i], across)
-        for i in range(CHUNKS):
-            a, b = i, (i + CHUNKS // 2) % CHUNKS
-            send(src_of(a), place(slot, a), recv_sems.at[base, a], up)
-            send(src_of(b), place(slot, b), recv_sems.at[base + 1, b], down)
-        for i in range(CHUNKS):
-            send(src_of(i), place(slot, i), recv_sems.at[sib_kind, i], sib)
-
-    launch(lambda i: feats.at[rows(i)], here.row, None, 0, True, 7)
-
+    slots_of = [here.slot(*column) for column in columns]
+    opposite = [(i + CHUNKS // 2) % CHUNKS for i in range(CHUNKS)]
+
+    for i in range(CHUNKS):
+        send(feats.at[rows(i)], place(here.row, i), recv_sems.at[3, i], across)
+    for a, b in enumerate(opposite):
+        send(feats.at[rows(a)], place(here.row, a), recv_sems.at[0, a], up)
+        send(feats.at[rows(b)], place(here.row, b), recv_sems.at[1, b], down)
+    for i in range(CHUNKS):
+        send(feats.at[rows(i)], place(here.row, i), recv_sems.at[7, i], sib)
     mine = pl.ds(pl.multiple_of(here.c * half, half), half)
-    for d in range(1, N_REP):
-        q = peers[d - 1]
-        send(weight.at[mine], ws.at[here.rep, mine], w_recv.at[d - 1], (here.row, q))
-    for d in range(1, N_REP):
-        q = peers[d - 1]
+    theirs = pl.ds(pl.multiple_of((1 - here.c) * half, half), half)
+    for d, q in enumerate(peers):
+        send(weight.at[mine], ws.at[here.rep, mine], w_recv.at[d], (here.row, q))
+    for d, q in enumerate(peers):
         send(
             cot.at[pl.ds(pl.multiple_of(q * piece, piece), piece)],
-            cots.at[here.rep], cot_recv.at[d - 1], (here.row, q),
+            cots.at[here.rep], cot_recv.at[d], (here.row, q),
         )
-
-    stores = [
-        pltpu.make_async_copy(own, gathered.at[here.row], local_sems.at[3]),
-        pltpu.make_async_copy(own_w, ws.at[here.rep], local_sems.at[4]),
-        pltpu.make_async_copy(own_c, cots.at[here.rep], local_sems.at[5]),
-    ]
-    for load, store in zip(loads, stores):
-        load.wait()
-        store.start()
-
-    def take(kind, chunk, to_up, to_down):
-        slot = slots[kind]
-        arrived(place(slot, chunk), recv_sems.at[kind, chunk])
-        far = 2 if kind < 3 else 6
-        if to_up:
-            send(place(slot, chunk), place(slot, chunk), recv_sems.at[far, chunk], up)
-        if to_down:
-            send(place(slot, chunk), place(slot, chunk), recv_sems.at[far, chunk], down)
-        send(place(slot, chunk), place(slot, chunk), recv_sems.at[8 + kind, chunk], sib)
-
-    for base in (0, 4):
+    for copy in own:
+        copy.start()
+
+    def take(kind, chunk, on=None):
+        src = place(slots_of[kind], chunk)
+        arrived(src, recv_sems.at[kind, chunk])
+        if on is not None:
+            send(src, src, recv_sems.at[2 if kind < 3 else 6, chunk], on)
+        send(src, src, recv_sems.at[8 + kind, chunk], sib)
+
+    for k in (0, 4):
+        for a, b in enumerate(opposite):
+            take(k, a, up if a < CHUNKS // 2 else None)
+            take(k + 1, b, down if b >= CHUNKS // 2 else None)
+            if k == 0:
+                src = place(slots_of[3], a)
+                arrived(src, recv_sems.at[3, a])
+                send(src, src, recv_sems.at[4, a], up)
+                send(src, src, recv_sems.at[5, a], down)
+                send(src, src, recv_sems.at[11, a], sib)
         for i in range(CHUNKS):
-            a, b = i, (i + CHUNKS // 2) % CHUNKS
-            take(base, a, a < CHUNKS // 2, False)
-            take(base + 1, b, False, b >= CHUNKS // 2)
-            if base == 0:
-                arrived(place(slots[3], i), recv_sems.at[3, i])
-                src = place(slots[3], i)
-                send(src, src, recv_sems.at[4, i], up)
-                send(src, src, recv_sems.at[5, i], down)
-                send(src, src, recv_sems.at[11, i], sib)
+            take(k + 2, i)
+        if k == 0:
+            for d, q in enumerate(peers):
+                arrived(ws.at[q, mine], w_recv.at[d])
+                send(ws.at[q, mine], ws.at[q, mine], w_sib.at[d], sib)
+
+    for d, q in enumerate(peers):
+        arrived(ws.at[q, theirs], w_sib.at[d])
+        arrived(cots.at[q], cot_recv.at[d])
+    for copy in own:
+        copy.wait()
+    for r in range(N_REP):
+        w[:, r * width : (r + 1) * width] = ws[r]
+    for kind, column in enumerate([(False, 0)] + columns):
         for i in range(CHUNKS):
-            take(2 if base == 0 else 6, i, False, False)
-        if base == 0:
-            for d in range(1, N_REP):
-                q = peers[d - 1]
-                arrived(ws.at[q, mine], w_recv.at[d - 1])
-                send(ws.at[q, mine], ws.at[q, mine], w_sib.at[d - 1], sib)
-
-    theirs = pl.ds(pl.multiple_of((1 - here.c) * half, half), half)
-    for d in range(1, N_REP):
-        q = peers[d - 1]
-        arrived(ws.at[q, theirs], w_sib.at[d - 1])
-        arrived(cots.at[q], cot_recv.at[d - 1])
-    sib_slots = [here.slot(False, 0, True)] + [
-        here.slot(other, dy, True)
-        for other, dy in ((False, -1), (False, 1), (False, 2), (True, 0), (True, -1), (True, 1), (True, 2))
-    ]
-    for kind in range(8):
-        for i in range(CHUNKS):
-            arrived(place(sib_slots[kind], i), recv_sems.at[7 + kind, i])
-    for store in stores:
-        store.wait()
-    send.finish()
-
-
-def gather_all(features, cotangent, weight):
-    rows, width = features.shape
-    n_sends = 15 * CHUNKS + 21
-    return pl.pallas_call(
-        gather_kernel,
-        in_specs=[ANY] * 3,
-        out_specs=[ANY] * 3,
-        out_shape=[
-            jax.ShapeDtypeStruct((N_ROW, rows, width), BF16),
-            jax.ShapeDtypeStruct((N_REP, rows // N_REP, width), BF16),
-            jax.ShapeDtypeStruct((N_REP,) + weight.shape, BF16),
-        ],
-        scratch_shapes=[
-            pltpu.VMEM((rows, width), BF16),
-            pltpu.VMEM(weight.shape, BF16),
-            pltpu.VMEM((rows // N_REP, width), BF16),
-            pltpu.SemaphoreType.DMA((n_sends,)),
-            pltpu.SemaphoreType.DMA((15, CHUNKS)),
-            pltpu.SemaphoreType.DMA((N_REP - 1,)),
-            pltpu.SemaphoreType.DMA((N_REP - 1,)),
-            pltpu.SemaphoreType.DMA((N_REP - 1,)),
-            pltpu.SemaphoreType.DMA((6,)),
-        ],
-        compiler_params=pltpu.CompilerParams(collective_id=0, has_side_effects=True),
-        name="gather_all",
-    )(features, cotangent, weight)
-
-
-STRIP = 128
-
-
-def dense_kernel(
-    mixed, cots, ws, mixed_grad, act, wgrad, m, w, cot, grad, back,
-    send_sems, m_recv, back_recv, local_sems,
-):
-    here = Place()
-    piece, width = mixed.shape[1:]
-    peers = [here.peer(d) for d in range(1, N_REP)]
-    first = pltpu.make_async_copy(mixed.at[here.rep], m.at[here.rep], local_sems.at[0])
-    first.start()
-    loads = []
-    for r in range(N_REP):
-        at = pl.ds(r * width, width)
-        loads.append(pltpu.make_async_copy(ws.at[r], w.at[:, at], local_sems.at[1 + r]))
-        loads.append(pltpu.make_async_copy(cots.at[r], cot.at[:, at], local_sems.at[9 + r]))
-    greet([(here.row, q) for q in peers])
-    send = Sends(send_sems)
-    for d, q in enumerate(peers):
-        send(mixed.at[q], m.at[here.rep], m_recv.at[d], (here.row, q))
-    for load in loads:
-        load.start()
-    for load in loads:
-        load.wait()
-    first.wait()
+            arrived(place(here.slot(*column, True), i), recv_sems.at[7 + kind, i])
+
+    def mix(dst, q):
+        @pl.loop(0, piece // (t * PAIR))
+        def _(j):
+            for e in range(PAIR):
+                i = j * PAIR + e
+                b = q * (piece // t) + i
+                n = counts[b]
+                left = jnp.concatenate(
+                    [jnp.where(k < n, blocks[b, k], jnp.zeros((), BF16)) for k in range(slots)],
+                    axis=1,
+                )
+                right = jnp.concatenate([full[cols[k, b]] for k in range(slots)], axis=0)
+                dst[pl.ds(pl.multiple_of(i * t, t), t), :] = jnp.dot(
+                    left, right, preferred_element_type=F32
+                ).astype(BF16)
+
+    def shift(d):
+        q = here.peer_at(d)
+        return q, pltpu.make_async_remote_copy(
+            src_ref=mixed.at[q], dst_ref=m.at[here.rep],
+            send_sem=m_send.at[d - 1], recv_sem=m_recv.at[d - 1],
+            device_id=(here.row, q), device_id_type=MESH,
+        )
+
+    @pl.loop(1, N_REP)
+    def _(d):
+        q, copy = shift(d)
+        mix(mixed.at[q], q)
+        copy.start()
+
+    mix(m.at[here.rep], here.rep)
     for d, q in enumerate(peers):
         arrived(m.at[q], m_recv.at[d])
 
     for i in range(piece // STRIP):
-        rows = pl.ds(i * STRIP, STRIP)
-        x = jnp.concatenate([m[r, rows, :] for r in range(N_REP)], axis=1)
+        at = pl.ds(i * STRIP, STRIP)
+        x = jnp.concatenate([m[r, at, :] for r in range(N_REP)], axis=1)
+        c = jnp.concatenate([cots[r, at, :] for r in range(N_REP)], axis=1)
         pre = jnp.dot(x, w[...], preferred_element_type=F32)
         sig = jax.nn.sigmoid(pre)
         out = (pre * sig).astype(BF16)
-        g = (cot[rows, :].astype(F32) * sig * (1.0 + pre * (1.0 - sig))).astype(BF16)
-        grad[rows, :] = g
+        g = (c.astype(F32) * sig * (1.0 + pre * (1.0 - sig))).astype(BF16)
+        grad[at, :] = g
         b = lax.dot_general(
             g, w[...], (((1,), (1,)), ((), ())), preferred_element_type=F32
         ).astype(BF16)
         for r in range(N_REP):
-            act[r, rows, :] = out[:, r * width : (r + 1) * width]
-            back[r, rows, :] = b[:, r * width : (r + 1) * width]
+            act[r, at, :] = out[:, r * width : (r + 1) * width]
+            back[r, at, :] = b[:, r * width : (r + 1) * width]
         for d, q in enumerate(peers):
-            send(
-                back.at[q, rows], mixed_grad.at[here.rep, rows], back_recv.at[d, i],
-                (here.row, q),
-            )
-    last = pltpu.make_async_copy(back.at[here.rep], mixed_grad.at[here.rep], local_sems.at[0])
+            send(back.at[q, at], mixed_grad.at[here.rep, at], back_recv.at[d, i], (here.row, q))
+    last = pltpu.make_async_copy(back.at[here.rep], mixed_grad.at[here.rep], local_sems.at[4])
     last.start()
     for r in range(N_REP):
         wgrad[r] = lax.dot_general(
@@ -282,35 +248,45 @@
     for d, q in enumerate(peers):
         for i in range(piece // STRIP):
             arrived(mixed_grad.at[q, pl.ds(i * STRIP, STRIP)], back_recv.at[d, i])
+    for d in range(1, N_REP):
+        shift(d)[1].wait_send()
     send.finish()
 
 
-def dense(mixed, cots, ws):
-    n, piece, width = mixed.shape
+def forward(features, cotangent, weight, tiles, columns, counts):
+    rows, width = features.shape
+    n_blocks, _, t, _ = tiles.shape
+    piece = rows // N_REP
     strips = piece // STRIP
+    dma = pltpu.SemaphoreType.DMA
+    smem = pl.BlockSpec(memory_space=pltpu.SMEM)
+    stack = pltpu.VMEM((N_REP, piece, width), BF16)
     return pl.pallas_call(
-        dense_kernel,
-        in_specs=[ANY] * 3,
+        forward_kernel,
+        in_specs=[ANY] * 4 + [smem] * 2,
         out_specs=[ANY, VM, VM],
         out_shape=[
-            jax.ShapeDtypeStruct(mixed.shape, BF16),
-            jax.ShapeDtypeStruct(mixed.shape, BF16),
-            jax.ShapeDtypeStruct((n, width, n * width), BF16),
+            jax.ShapeDtypeStruct((N_REP, piece, width), BF16),
+            jax.ShapeDtypeStruct((N_REP, piece, width), BF16),
+            jax.ShapeDtypeStruct((N_REP, width, N_REP * width), BF16),
         ],
         scratch_shapes=[
-            pltpu.VMEM((n, piece, width), BF16),
-            pltpu.VMEM((n * width, n * width), BF16),
-            pltpu.VMEM((piece, n * width), BF16),
-            pltpu.VMEM((piece, n * width), BF16),
-            pltpu.VMEM((n, piece, width), BF16),
-            pltpu.SemaphoreType.DMA(((n - 1) * (1 + strips),)),
-            pltpu.SemaphoreType.DMA((n - 1,)),
-            pltpu.SemaphoreType.DMA((n - 1, strips)),
-            pltpu.SemaphoreType.DMA((17,)),
+            pltpu.VMEM((N_ROW * n_blocks, t, width), BF16),
+            pltpu.VMEM(tiles.shape, BF16),
+            stack,
+            pltpu.VMEM((N_REP,) + weight.shape, BF16),
+            pltpu.VMEM((N_REP * width, N_REP * width), BF16),
+            stack, stack,
+            pltpu.VMEM((piece, N_REP * width), BF16),
+            stack,
+            dma((15 * CHUNKS + 21 + 7 * strips,)), dma((15, CHUNKS)),
+            dma((7,)), dma((7,)), dma((7,)), dma((7,)), dma((7,)), dma((7, strips)), dma((5,)),
         ],
-        compiler_params=pltpu.CompilerParams(collective_id=1, has_side_effects=True),
-        name="dense",
-    )(mixed, cots, ws)
+        compiler_params=pltpu.CompilerParams(
+            collective_id=0, has_side_effects=True, vmem_limit_bytes=60 * 1024 * 1024
+        ),
+        name="forward",
+    )(features.reshape(n_blocks, t, width), cotangent, weight, tiles, columns, counts)
 
 
 OFFSETS = (2, 1, -1, 0)
@@ -521,79 +497,6 @@
 SLOTS_AHEAD = 4
 
 
-def fwd_kernel(cols, counts, tiles, gathered, out, tbuf, gbuf, sems):
-    blocks, slots, t, _ = tiles.shape
-
-    def copies(b, k):
-        s = lax.rem(b, SLOTS_AHEAD)
-        at = pl.ds(pl.multiple_of(k * t, t), t)
-        return (
-            pltpu.make_async_copy(tiles.at[b, k], tbuf.at[s, :, at], sems.at[s, k, 0]),
-            pltpu.make_async_copy(gathered.at[cols[k, b]], gbuf.at[s, at, :], sems.at[s, k, 1]),
-        )
-
-    def start(b):
-        @pl.loop(0, counts[b])
-        def _(k):
-            for c in copies(b, k):
-                c.start()
-
-    for b in range(SLOTS_AHEAD - 1):
-        start(b)
-
-    @pl.loop(0, blocks)
-    def _(b):
-        s = lax.rem(b, SLOTS_AHEAD)
-
-        @pl.when(b + SLOTS_AHEAD - 1 < blocks)
-        def _():
-            start(b + SLOTS_AHEAD - 1)
-
-        n = counts[b]
-
-        @pl.loop(0, n)
-        def _(k):
-            for c in copies(b, k):
-                c.wait()
-
-        @pl.when(lax.rem(n, 2) == 1)
-        def _():
-            at = pl.ds(pl.multiple_of(n * t, t), t)
-            tbuf[s, :, at] = jnp.zeros((t, t), BF16)
-            gbuf[s, at, :] = jnp.zeros((t, t), BF16)
-
-        row = pl.ds(pl.multiple_of(b * t, t), t)
-        for p in range(1, slots // 2 + 1):
-
-            @pl.when((n + 1) // 2 == p)
-            def _():
-                w = 2 * p * t
-                out[row, :] = jnp.dot(
-                    tbuf[s, :, :w], gbuf[s, :w, :], preferred_element_type=F32
-                ).astype(BF16)
-
-
-def spmm(gathered, tiles, columns, counts):
-    blocks, slots, t, _ = tiles.shape
-    width = gathered.shape[-1]
-    return pl.pallas_call(
-        fwd_kernel,
-        grid_spec=pltpu.PrefetchScalarGridSpec(
-            num_scalar_prefetch=2,
-            grid=(1,),
-            in_specs=[pl.BlockSpec(memory_space=pl.ANY)] * 2,
-            out_specs=pl.BlockSpec((blocks * t, width), lambda i, *_: (0, 0)),
-            scratch_shapes=[
-                pltpu.VMEM((SLOTS_AHEAD, t, slots * t), BF16),
-                pltpu.VMEM((SLOTS_AHEAD, slots * t, width), BF16),
-                pltpu.SemaphoreType.DMA((SLOTS_AHEAD, slots, 2)),
-            ],
-        ),
-        out_shape=jax.ShapeDtypeStruct((blocks * t, width), BF16),
-        name="spmm",
-    )(columns, counts, tiles, gathered)
-
-
 GROUP = 4
 OUT_CHUNK = 16
 
@@ -710,10 +613,8 @@
     blocks_here, slots, t, _ = tiles.shape
     total_blocks = blocks_here * lax.axis_size("row")
     columns = columns.T
-    gathered, cots, ws = gather_all(features, cotangent, weight)
-    mixed = spmm(gathered.reshape(total_blocks, t, feat_local), tiles, columns, counts)
-    mixed_grad, act, wgrad = dense(mixed.reshape(N_REP, -1, feat_local), cots, ws)
-    part = spmm_t(mixed_grad.reshape(mixed.shape), tiles, columns, counts, total_blocks)
+    mixed_grad, act, wgrad = forward(features, cotangent, weight, tiles, columns, counts)
+    part = spmm_t(mixed_grad.reshape(features.shape), tiles, columns, counts, total_blocks)
     act, feature_grad, weight_grad = reduce_all(
         part.reshape(N_ROW, rows_here, feat_local), act, wgrad
     )

time: 257 us -> 235 us (0.914)
  Pallas kernels: 249 us -> 228 us
    pallas_call x3 -> x1, Pallas kernels: 138 us -> 117 us  [forward(): pl.pallas_call(forward_kernel, in_specs=[ANY] * 4 + [smem] * 2, out_specs...]
where the time goes in v5:
time: 235 us
  Pallas kernels  228 us (97%)
  local copies, waits for them, and re-layouts  6.06 us (3%)
    pallas_call x1, Pallas kernels, forward(): pl.pallas_call(forward_kernel, in_specs=[ANY] * 4 + [smem] * 2, out_specs...  117 us
    pallas_call x1, Pallas kernels, reduce_all(): pl.pallas_call(reduce_kernel, in_specs=[ANY] * 3, out_specs=[ANY, VM, VM]...  81.3 us
    pallas_call x1, Pallas kernels, spmm_t(): pl.pallas_call(bwd_kernel, grid_spec=pltpu.PrefetchScalarGridSpec(num_sca...  30.1 us
    unnamed x3, local copies, waits for them, and re-layouts  6.06 us

profile of v5, /device:TPU:1, one launch (start us, length us, event | category | flops | bytes accessed | tf_op | source)
XLA Modules:
  0.0 235.0 jit_solution(18225340123740836045)
XLA Ops:
  0.6 116.9 %forward.1 = (bf16[8,512,128]{2,1,0:T(8,128)(2,1)}, bf16[8,512,128]{2,1,0:T(8,128)(2,1)}, bf16[8,128,1024]{2,1,0:T(8,128)(2,1)}) custom-call(bf16[32,128,128]{2,1,0:T(8,128)(2,1)} %bitcast.6, bf16[4096,128]{1,0:T(8,128)(2,1)} %cot.1, bf16[1024,128]{1,0:T(8,128)(2,1)} %weight.1, bf16[32,16,128,128]{3,2,1,0:T(8,128)(2,1)} %tiles.3, s32[16,32]{1,0:T(8,128)} %bitcast.9, ...), custom_call_target="tpu_custom_call" | custom-call | tf_op jit(solution)/shard_map/forward/pallas_call | solution.py:264
  117.5 30.1 %spmm_t.1 = bf16[512,128,128]{2,1,0:T(8,128)(2,1)} custom-call(s32[16,32]{1,0:T(8,128)} %bitcast.10, s32[32]{0:T(128)} %counts.3, bf16[32,16,128,128]{3,2,1,0:T(8,128)(2,1)} %tiles.3, bf16[4096,128]{1,0:T(8,128)(2,1)} %bitcast.8), custom_call_target="tpu_custom_call" | custom-call | tf_op jit(solution)/shard_map/spmm_t/pallas_call | solution.py:587
  147.6 81.3 %reduce_all.1 = (bf16[8,512,128]{2,1,0:T(8,128)(2,1)}, bf16[4096,128]{1,0:T(8,128)(2,1)}, f32[128,64]{1,0:T(8,128)}) custom-call(bf16[16,4096,128]{2,1,0:T(8,128)(2,1)} %bitcast.5, bf16[8,512,128]{2,1,0:T(8,128)(2,1)} %get-tuple-element.10.act, bf16[8,128,1024]{2,1,0:T(8,128)(2,1)} %get-tuple-element.11.wgrad), custom_call_target="tpu_custom_call" | custom-call | tf_op jit(solution)/shard_map/reduce_all/pallas_call | solution.py:464
  229.0 1.5 copy.9
  230.5 2.3 copy.12
  232.8 2.3 copy.13

commit v6 on v5

--- a/solution.py
+++ b/solution.py
@@ -85,6 +85,7 @@
 
 
 CHUNKS = 4
+CROSS = 0
 
 
 STRIP = 128
@@ -157,17 +158,20 @@
         arrived(src, recv_sems.at[kind, chunk])
         if on is not None:
             send(src, src, recv_sems.at[2 if kind < 3 else 6, chunk], on)
+        if kind < 3 and chunk == CROSS:
+            send(src, src, recv_sems.at[4 + kind, chunk], across)
         send(src, src, recv_sems.at[8 + kind, chunk], sib)
 
     for k in (0, 4):
         for a, b in enumerate(opposite):
-            take(k, a, up if a < CHUNKS // 2 else None)
-            take(k + 1, b, down if b >= CHUNKS // 2 else None)
+            take(k, a, up if a < CHUNKS // 2 and (k, a) != (4, CROSS) else None)
+            take(k + 1, b, down if b >= CHUNKS // 2 and (k, b) != (4, CROSS) else None)
             if k == 0:
                 src = place(slots_of[3], a)
                 arrived(src, recv_sems.at[3, a])
-                send(src, src, recv_sems.at[4, a], up)
-                send(src, src, recv_sems.at[5, a], down)
+                if a != CROSS:
+                    send(src, src, recv_sems.at[4, a], up)
+                    send(src, src, recv_sems.at[5, a], down)
                 send(src, src, recv_sems.at[11, a], sib)
         for i in range(CHUNKS):
             take(k + 2, i)
@@ -212,8 +216,8 @@
         )
 
     @pl.loop(1, N_REP)
-    def _(d):
-        q, copy = shift(d)
+    def _(e):
+        q, copy = shift(lax.rem(3 * e, N_REP))
         mix(mixed.at[q], q)
         copy.start()
 
@@ -295,9 +299,9 @@
 
 def reduce_kernel(
     part, act, wgrad, act_out, out, wg_out,
-    own, theirs, far_up, far_down, near_up, near_down, cross, own_act,
-    wg_in, wg_sum, wg_sib, wg_half, wg_row, wg_fin, wg_fin_sib,
-    send_sems, load_sems, sib_recv, far_recv, near_recv, cross_recv,
+    own, theirs, far_up, far_down, near_up, near_down, cross, early, own_act,
+    wg_own, wg_sib, wg_in, wg_half, wg_row, wg_fin, wg_fin_sib,
+    send_sems, load_sems, sib_recv, far_recv, near_recv, cross_recv, early_recv,
     act_recv, wg_recv, row_recv, pair_recv, local_sems,
 ):
     here = Place()
@@ -308,6 +312,10 @@
     up, down, across = here.at(False, 1), here.at(False, -1), here.at(True, 0)
     columns = [(o, dy) for o in (True, False) for dy in OFFSETS][:-1]
 
+    edge = wg_half.shape[1]
+    mine = pl.ds(pl.multiple_of(here.c * edge, edge), edge)
+    theirs_of_pair = pl.ds(pl.multiple_of((1 - here.c) * edge, edge), edge)
+
     def rows(i):
         return pl.ds(i * step, step)
 
@@ -320,7 +328,7 @@
             )
     extra = [
         pltpu.make_async_copy(act.at[here.rep], own_act, local_sems.at[0]),
-        pltpu.make_async_copy(wgrad.at[here.rep], wg_in.at[N_REP - 1], local_sems.at[1]),
+        pltpu.make_async_copy(wgrad.at[:, mine], wg_own, local_sems.at[1]),
     ]
     for load in extra:
         load.start()
@@ -329,11 +337,13 @@
     greet([sib] + [here.at(*column) for column in columns] + [(here.row, q) for q in peers])
 
     send = Sends(send_sems)
-    order = [0, 4, 1, 2, 3, 5, 6, 7]
-    for r in order:
+    first = [(0, i) for i in range(CHUNKS)] + [(r, CROSS) for r in (1, 2, 3)]
+    rest = [(r, i) for r in (1, 2, 4, 3, 5, 6, 7) for i in range(CHUNKS)]
+    for r, i in first + [k for k in rest if k not in first]:
         slot = here.slot(r < 4, OFFSETS[r % 4], True)
-        for i in range(CHUNKS):
-            send(part.at[slot, rows(i)], theirs.at[r, rows(i)], sib_recv.at[r, i], sib)
+        send(part.at[slot, rows(i)], theirs.at[r, rows(i)], sib_recv.at[r, i], sib)
+        if (r, i) == first[-1]:
+            send(wgrad.at[:, theirs_of_pair], wg_sib, pair_recv.at[0], sib)
 
     def total(r, i, more, dst=None):
         loads[r, i].wait()
@@ -347,37 +357,55 @@
             for ref, base in more:
                 at2 = pl.ds(pl.multiple_of(base * step + j * SUM_ROWS, SUM_ROWS), SUM_ROWS)
                 acc = acc + ref[at2, :].astype(F32)
+            if dst is not None:
+                acc = acc.T
             target[at, :] = acc.astype(BF16)
 
+    def plus(hh, k, i, more):
+        if hh == 1 and i == CROSS:
+            arrived(early.at[k], early_recv.at[k])
+            return more + [(early.at[k], 0)]
+        return more
+
+    def skip(hh, i):
+        return hh == 0 and i == CROSS
+
     def far(hh):
-        for i in range(half):
-            total(4 * hh, i, [])
-            send(own.at[4 * hh, rows(i)], far_up.at[hh, rows(i)], far_recv.at[hh, 0, i], up)
-            total(4 * hh, i + half, [])
-            send(
-                own.at[4 * hh, rows(i + half)], far_down.at[hh, rows(i)],
-                far_recv.at[hh, 1, i], down,
-            )
+        r = 4 * hh
+        for i in (1, 0):
+            for j, land, to in ((i, far_up, up), (i + half, far_down, down)):
+                if skip(hh, j):
+                    continue
+                total(r, j, plus(hh, 0, j, []))
+                send(
+                    own.at[r, rows(j)], land.at[hh, rows(i)],
+                    far_recv.at[hh, int(j >= half), i], to,
+                )
 
     def near(hh, i, j, up_more, down_more):
         r, s = 4 * hh + 1, 4 * hh + 2
-        total(r, i, up_more)
-        send(own.at[r, rows(i)], near_up.at[hh, rows(i)], near_recv.at[hh, 0, i], up)
-        total(s, j, down_more)
-        send(own.at[s, rows(j)], near_down.at[hh, rows(j)], near_recv.at[hh, 1, j], down)
+        if not skip(hh, i):
+            total(r, i, plus(hh, 1, i, up_more))
+            send(own.at[r, rows(i)], near_up.at[hh, rows(i)], near_recv.at[hh, 0, i], up)
+        if not skip(hh, j):
+            total(s, j, plus(hh, 2, j, down_more))
+            send(own.at[s, rows(j)], near_down.at[hh, rows(j)], near_recv.at[hh, 1, j], down)
 
     def near_first(hh):
-        for i in range(half):
+        for i in (1, 0):
             near(hh, i + half, i, [], [])
 
     def near_last(hh):
-        for i in range(half):
-            arrived(far_up.at[hh, rows(i)], far_recv.at[hh, 0, i])
+        for i in (1, 0):
+            if not skip(hh, i):
+                arrived(far_up.at[hh, rows(i)], far_recv.at[hh, 0, i])
             arrived(far_down.at[hh, rows(i)], far_recv.at[hh, 1, i])
             near(hh, i, i + half, [(far_up.at[hh], i)], [(far_down.at[hh], i)])
 
     def final(hh):
-        for i in [k + part for k in range(half) for part in (0, half)]:
+        for i in (3, 1, 2, 0):
+            if skip(hh, i):
+                continue
             arrived(near_up.at[hh, rows(i)], near_recv.at[hh, 0, i])
             arrived(near_down.at[hh, rows(i)], near_recv.at[hh, 1, i])
             more = [(near_up.at[hh], i), (near_down.at[hh], i)]
@@ -389,42 +417,44 @@
                 total(7, i, more + [(cross, i)], out)
 
     far(0)
-    for d, q in enumerate(peers):
-        send(wgrad.at[q], wg_in.at[d], wg_recv.at[d], (here.row, q))
+    for k in range(4):
+        total(k, CROSS, [])
+        if k < 3:
+            send(own.at[k, rows(CROSS)], early.at[k], early_recv.at[k], across)
+        else:
+            send(own.at[k, rows(CROSS)], cross.at[rows(CROSS)], cross_recv.at[CROSS], across)
+    near_first(0)
+
+    extra[1].wait()
+    arrived(wg_sib, pair_recv.at[0])
+
+    @pl.loop(0, N_REP)
+    def _(j):
+        wg_own[j] = (wg_own[j].astype(F32) + wg_sib[j].astype(F32)).astype(BF16)
+
+    for d, q in enumerate(peers):
+        send(wg_own.at[q], wg_in.at[d], wg_recv.at[d], (here.row, q))
     for d, q in enumerate(peers):
         send(act.at[q], act_out.at[here.rep], act_recv.at[d], (here.row, q))
     extra[0].wait()
     keep = pltpu.make_async_copy(own_act, act_out.at[here.rep], local_sems.at[0])
     keep.start()
-    near_first(0)
     far(1)
     near_last(0)
     near_first(1)
     final(0)
-
-    extra[1].wait()
+    near_last(1)
+
     for d in range(N_REP - 1):
         arrived(wg_in.at[d], wg_recv.at[d])
-    wide = wg_in.shape[2]
-    edge = wg_half.shape[1]
-
-    @pl.loop(0, wide // 128)
+
+    @pl.loop(0, wg_half.shape[0])
     def _(j):
         at = pl.ds(pl.multiple_of(j * 128, 128), 128)
-        acc = wg_in[0, :, at].astype(F32)
-        for d in range(1, N_REP):
+        acc = wg_own[here.rep, :, at].astype(F32)
+        for d in range(N_REP - 1):
             acc = acc + wg_in[d, :, at].astype(F32)
-        acc = acc.astype(BF16)
-        wg_sum[0, j] = acc[:edge]
-        wg_sum[1, j] = acc[edge:]
-
-    send(wg_sum.at[1 - here.c], wg_sib, pair_recv.at[0], sib)
-    near_last(1)
-    arrived(wg_sib, pair_recv.at[0])
-
-    @pl.loop(0, wide // 128)
-    def _(j):
-        wg_half[j] = (wg_sum[here.c, j].astype(F32) + wg_sib[j].astype(F32)).astype(BF16)
+        wg_half[j] = acc.astype(BF16)
 
     for k, (o, dy) in enumerate(columns):
         send(
@@ -478,16 +508,17 @@
             pltpu.VMEM((2, rows, width), BF16),
             pltpu.VMEM((2, rows, width), BF16),
             pltpu.VMEM((rows, width), BF16),
+            pltpu.VMEM((3, rows // CHUNKS, width), BF16),
             pltpu.VMEM(act.shape[1:], BF16),
-            pltpu.VMEM(wgrad.shape, BF16),
-            pltpu.VMEM((2, wide // 128, edge, 128), BF16),
-            pltpu.VMEM((wide // 128, edge, 128), BF16),
+            pltpu.VMEM((n_rep, edge, wide), BF16),
+            pltpu.VMEM((n_rep, edge, wide), BF16),
+            pltpu.VMEM((n_rep - 1, edge, wide), BF16),
             pltpu.VMEM((wide // 128, edge, 128), BF16),
             pltpu.VMEM((7, edge, 128), BF16),
             pltpu.VMEM((edge, 128), F32),
             pltpu.VMEM((edge, 128), F32),
             dma((15 * CHUNKS + 23,)), dma((8, CHUNKS)), dma((8, CHUNKS)), dma((2, 2, CHUNKS // 2)), dma((2, 2, CHUNKS)),
-            dma((CHUNKS,)), dma((7,)), dma((7,)), dma((7,)), dma((2,)), dma((2,)),
+            dma((CHUNKS,)), dma((3,)), dma((7,)), dma((7,)), dma((7,)), dma((2,)), dma((2,)),
         ],
         compiler_params=pltpu.CompilerParams(collective_id=2, has_side_effects=True),
         name="reduce_all",
@@ -539,19 +570,17 @@
 
             @pl.when((n + GROUP - 1) // GROUP == live)
             def _():
-                g = grad[pl.ds(pl.multiple_of(b * t, t), t), :]
+                g = grad[pl.ds(pl.multiple_of(b * t, t), t), :].T
                 for q in range(live):
                     copy(b, q).wait()
                 for q in range(live):
                     wide = jnp.concatenate(
                         [tbuf[s, q * GROUP + i] for i in range(GROUP)], axis=1
                     )
-                    terms = lax.dot_general(
-                        wide, g, (((0,), (0,)), ((), ())), preferred_element_type=F32
-                    )
+                    terms = jnp.dot(g, wide, preferred_element_type=F32)
                     for i in range(GROUP):
                         k = q * GROUP + i
-                        term = terms[i * t : (i + 1) * t]
+                        term = terms[:, i * t : (i + 1) * t]
                         if q == live - 1 and i > 0:
                             term = jnp.where(k < n, term, 0.0)
                         acc[cols[k, b]] += term

time: 235 us -> 229 us (0.974)
  Pallas kernels: 228 us -> 222 us
    pallas_call x1, Pallas kernels: 117 us -> 111 us  [forward(): pl.pallas_call(forward_kernel, in_specs=[ANY] * 4 + [smem] * 2, out_specs...]
where the time goes in v6:
time: 229 us; the launch traced here: 228 us
  Pallas kernels  222 us (97%)
  local copies, waits for them, and re-layouts  6.06 us (3%)
    pallas_call x1, Pallas kernels, forward(): pl.pallas_call(forward_kernel, in_specs=[ANY] * 4 + [smem] * 2, out_specs...  111 us
    pallas_call x1, Pallas kernels, reduce_all(): pl.pallas_call(reduce_kernel, in_specs=[ANY] * 3, out_specs=[ANY, VM, VM]...  80.5 us
    pallas_call x1, Pallas kernels, spmm_t(): pl.pallas_call(bwd_kernel, grid_spec=pltpu.PrefetchScalarGridSpec(num_sca...  30.4 us
    unnamed x3, local copies, waits for them, and re-layouts  6.06 us

profile of v6, /device:TPU:1, one launch (start us, length us, event | category | flops | bytes accessed | tf_op | source)
XLA Modules:
  0.0 228.3 jit_solution(4439148562192432584)
XLA Ops:
  0.6 110.7 %forward.1 = (bf16[8,512,128]{2,1,0:T(8,128)(2,1)}, bf16[8,512,128]{2,1,0:T(8,128)(2,1)}, bf16[8,128,1024]{2,1,0:T(8,128)(2,1)}) custom-call(bf16[32,128,128]{2,1,0:T(8,128)(2,1)} %bitcast.6, bf16[4096,128]{1,0:T(8,128)(2,1)} %cot.1, bf16[1024,128]{1,0:T(8,128)(2,1)} %weight.1, bf16[32,16,128,128]{3,2,1,0:T(8,128)(2,1)} %tiles.3, s32[16,32]{1,0:T(8,128)} %bitcast.9, ...), custom_call_target="tpu_custom_call" | custom-call | tf_op jit(solution)/shard_map/forward/pallas_call | solution.py:268
  111.3 30.4 %spmm_t.1 = bf16[512,128,128]{2,1,0:T(8,128)(2,1)} custom-call(s32[16,32]{1,0:T(8,128)} %bitcast.10, s32[32]{0:T(128)} %counts.3, bf16[32,16,128,128]{3,2,1,0:T(8,128)(2,1)} %tiles.3, bf16[4096,128]{1,0:T(8,128)(2,1)} %bitcast.8), custom_call_target="tpu_custom_call" | custom-call | tf_op jit(solution)/shard_map/spmm_t/pallas_call | solution.py:616
  141.7 80.5 %reduce_all.1 = (bf16[8,512,128]{2,1,0:T(8,128)(2,1)}, bf16[4096,128]{1,0:T(8,128)(2,1)}, f32[128,64]{1,0:T(8,128)}) custom-call(bf16[16,4096,128]{2,1,0:T(8,128)(2,1)} %bitcast.5, bf16[8,512,128]{2,1,0:T(8,128)(2,1)} %get-tuple-element.10.act, bf16[8,128,1024]{2,1,0:T(8,128)(2,1)} %get-tuple-element.11.wgrad), custom_call_target="tpu_custom_call" | custom-call | tf_op jit(solution)/shard_map/reduce_all/pallas_call | solution.py:494
  222.2 1.5 copy.9
  223.8 2.3 copy.12
  226.0 2.3 copy.13

commit v7 on v6

--- a/solution.py
+++ b/solution.py
@@ -441,9 +441,6 @@
     keep.start()
     far(1)
     near_last(0)
-    near_first(1)
-    final(0)
-    near_last(1)
 
     for d in range(N_REP - 1):
         arrived(wg_in.at[d], wg_recv.at[d])
@@ -460,6 +457,9 @@
         send(
             wg_half.at[here.slot(o, dy) // 2], wg_row.at[k], row_recv.at[k], here.at(o, dy)
         )
+    near_first(1)
+    final(0)
+    near_last(1)
     for k in range(len(columns)):
         arrived(wg_row.at[k], row_recv.at[k])
     acc = wg_half[here.row // 2].astype(F32)
@@ -525,11 +525,12 @@
     )(part, act, wgrad)
 
 
-SLOTS_AHEAD = 4
+SLOTS_AHEAD = 8
 
 
 GROUP = 4
 OUT_CHUNK = 16
+FLUSHES = 8
 
 
 def bwd_kernel(cols, counts, tiles, grad, out, acc, tbuf, stage, sems, out_sems):
@@ -586,18 +587,18 @@
                         acc[cols[k, b]] += term
 
     def flush(c):
-        s = lax.rem(c, 2)
+        s = lax.rem(c, FLUSHES)
         return pltpu.make_async_copy(
             stage.at[s], out.at[pl.ds(c * OUT_CHUNK, OUT_CHUNK)], out_sems.at[s]
         )
 
     @pl.loop(0, total // OUT_CHUNK)
     def _(c):
-        s = lax.rem(c, 2)
-
-        @pl.when(c >= 2)
+        s = lax.rem(c, FLUSHES)
+
+        @pl.when(c >= FLUSHES)
         def _():
-            flush(c - 2).wait()
+            flush(c - FLUSHES).wait()
 
         @pl.loop(0, OUT_CHUNK // 4)
         def _(j):
@@ -606,7 +607,7 @@
 
         flush(c).start()
 
-    for c in (total // OUT_CHUNK - 2, total // OUT_CHUNK - 1):
+    for c in range(total // OUT_CHUNK - FLUSHES, total // OUT_CHUNK):
         flush(c).wait()
 
 
@@ -626,15 +627,52 @@
             scratch_shapes=[
                 pltpu.VMEM((total, t, width), F32),
                 pltpu.VMEM((SLOTS_AHEAD, slots, t, t), BF16),
-                pltpu.VMEM((2, OUT_CHUNK, t, width), BF16),
+                pltpu.VMEM((FLUSHES, OUT_CHUNK, t, width), BF16),
                 pltpu.SemaphoreType.DMA((SLOTS_AHEAD, slots // GROUP)),
-                pltpu.SemaphoreType.DMA((2,)),
+                pltpu.SemaphoreType.DMA((FLUSHES,)),
             ],
         ),
         out_shape=jax.ShapeDtypeStruct((total, t, width), BF16),
         compiler_params=pltpu.CompilerParams(vmem_limit_bytes=60 * 1024 * 1024),
         name="spmm_t",
     )(columns, counts, tiles, grad)
+
+
+PARTS = 4
+
+
+def settle_kernel(a, b, w, a_out, b_out, w_out, a_buf, b_buf, in_sems, out_sems):
+    step = a.shape[0] // PARTS
+    ins, outs = [], []
+    for j, (src, buf, dst) in enumerate(((a, a_buf, a_out), (b, b_buf, b_out))):
+        for i in range(PARTS):
+            at = pl.ds(i * step, step)
+            ins.append(pltpu.make_async_copy(src.at[at], buf.at[at], in_sems.at[j, i]))
+            outs.append(pltpu.make_async_copy(buf.at[at], dst.at[at], out_sems.at[j, i]))
+    for copy in ins:
+        copy.start()
+    w_out[...] = w[...].T
+    for first, then in zip(ins, outs):
+        first.wait()
+        then.start()
+    for copy in outs:
+        copy.wait()
+
+
+def settle(a, b, w):
+    dma = pltpu.SemaphoreType.DMA((2, PARTS))
+    return pl.pallas_call(
+        settle_kernel,
+        in_specs=[ANY, ANY, VM],
+        out_specs=[ANY, ANY, VM],
+        out_shape=[
+            jax.ShapeDtypeStruct(a.shape, BF16),
+            jax.ShapeDtypeStruct(b.shape, BF16),
+            jax.ShapeDtypeStruct(w.shape[::-1], F32),
+        ],
+        scratch_shapes=[pltpu.VMEM(a.shape, BF16), pltpu.VMEM(b.shape, BF16), dma, dma],
+        name="settle",
+    )(a, b, w)
 
 
 def local(features, tiles, columns, counts, weight, cotangent):
@@ -647,7 +685,8 @@
     act, feature_grad, weight_grad = reduce_all(
         part.reshape(N_ROW, rows_here, feat_local), act, wgrad
     )
-    return act.reshape(features.shape), feature_grad, weight_grad
+    act, feature_grad, weight_grad = settle(act.reshape(features.shape), feature_grad, weight_grad)
+    return act, feature_grad, weight_grad.T
 
 
 def solution(mesh):

time: 229 us -> 216 us (0.943)
  Pallas kernels: 222 us -> 215 us
  local copies, waits for them, and re-layouts: 6.06 us -> 0 us
    pallas_call x1, Pallas kernels: 30.4 us -> 22.2 us  [spmm_t(): pl.pallas_call(bwd_kernel, grid_spec=pltpu.PrefetchScalarGridSpec(num_sca...]
    unnamed x3 -> x0, local copies, waits for them, and re-layouts: 6.06 us -> none
    pallas_call x0 -> x1, Pallas kernels: none -> 3.85 us  [settle(): pl.pallas_call(settle_kernel, in_specs=[ANY, ANY, VM], out_specs=[ANY, AN...]
    pallas_call x1, Pallas kernels: 80.5 us -> 77.9 us  [reduce_all(): pl.pallas_call(reduce_kernel, in_specs=[ANY] * 3, out_specs=[ANY, VM, VM]...]
where the time goes in v7:
time: 216 us; the launch traced here: 215 us
  Pallas kernels  215 us (100%)
    pallas_call x1, Pallas kernels, forward(): pl.pallas_call(forward_kernel, in_specs=[ANY] * 4 + [smem] * 2, out_specs...  111 us
    pallas_call x1, Pallas kernels, reduce_all(): pl.pallas_call(reduce_kernel, in_specs=[ANY] * 3, out_specs=[ANY, VM, VM]...  77.9 us
    pallas_call x1, Pallas kernels, spmm_t(): pl.pallas_call(bwd_kernel, grid_spec=pltpu.PrefetchScalarGridSpec(num_sca...  22.2 us

profile of v7, /device:TPU:1, one launch (start us, length us, event | category | flops | bytes accessed | tf_op | source)
XLA Modules:
  0.0 215.3 jit_solution(14153576547669238204)
XLA Ops:
  0.6 110.7 %forward.1 = (bf16[8,512,128]{2,1,0:T(8,128)(2,1)}, bf16[8,512,128]{2,1,0:T(8,128)(2,1)}, bf16[8,128,1024]{2,1,0:T(8,128)(2,1)}) custom-call(bf16[32,128,128]{2,1,0:T(8,128)(2,1)} %bitcast.7, bf16[4096,128]{1,0:T(8,128)(2,1)} %cot.1, bf16[1024,128]{1,0:T(8,128)(2,1)} %weight.1, bf16[32,16,128,128]{3,2,1,0:T(8,128)(2,1)} %tiles.3, s32[16,32]{1,0:T(8,128)} %bitcast.10, ...), custom_call_target="tpu_custom_call" | custom-call | tf_op jit(solution)/shard_map/forward/pallas_call | solution.py:268
  111.3 22.2 %spmm_t.1 = bf16[512,128,128]{2,1,0:T(8,128)(2,1)} custom-call(s32[16,32]{1,0:T(8,128)} %bitcast.11, s32[32]{0:T(128)} %counts.3, bf16[32,16,128,128]{3,2,1,0:T(8,128)(2,1)} %tiles.3, bf16[4096,128]{1,0:T(8,128)(2,1)} %bitcast.9), custom_call_target="tpu_custom_call" | custom-call | tf_op jit(solution)/shard_map/spmm_t/pallas_call | solution.py:617
  133.5 77.9 %reduce_all.1 = (bf16[8,512,128]{2,1,0:T(8,128)(2,1)}, bf16[4096,128]{1,0:T(8,128)(2,1)}, f32[128,64]{1,0:T(8,128)}) custom-call(bf16[16,4096,128]{2,1,0:T(8,128)(2,1)} %bitcast.6, bf16[8,512,128]{2,1,0:T(8,128)(2,1)} %get-tuple-element.13.act, bf16[8,128,1024]{2,1,0:T(8,128)(2,1)} %get-tuple-element.14.wgrad), custom_call_target="tpu_custom_call" | custom-call | tf_op jit(solution)/shard_map/reduce_all/pallas_call | solution.py:494
  211.4 3.8 %settle.1 = (bf16[4096,128]{1,0:T(8,128)(2,1)}, bf16[4096,128]{1,0:T(8,128)(2,1)}, f32[64,128]{1,0:T(8,128)}) custom-call(bf16[4096,128]{1,0:T(8,128)(2,1)} %bitcast.8, bf16[4096,128]{1,0:T(8,128)(2,1)} %get-tuple-element.16.b, f32[128,64]{1,0:T(8,128)} %get-tuple-element.17.w), custom_call_target="tpu_custom_call" | custom-call | tf_op jit(solution)/shard_map/settle/pallas_call | solution.py:664

commit v8 on v7

--- a/solution.py
+++ b/solution.py
@@ -88,7 +88,6 @@
 CROSS = 0
 
 
-STRIP = 128
 PAIR = 2
 
 
@@ -191,42 +190,47 @@
         for i in range(CHUNKS):
             arrived(place(here.slot(*column, True), i), recv_sems.at[7 + kind, i])
 
-    def mix(dst, q):
-        @pl.loop(0, piece // (t * PAIR))
+    strips = piece // t
+
+    def shift(d, i):
+        q, at = here.peer_at(d), pl.ds(i * t, t)
+        return q, pltpu.make_async_remote_copy(
+            src_ref=mixed.at[q, at], dst_ref=m.at[here.rep, at],
+            send_sem=m_send.at[d - 1, i], recv_sem=m_recv.at[d - 1, i],
+            device_id=(here.row, q), device_id_type=MESH,
+        )
+
+    def mix(i):
+        at = pl.ds(i * t, t)
+
+        @pl.loop(0, N_REP // PAIR)
         def _(j):
+            copies = []
             for e in range(PAIR):
-                i = j * PAIR + e
-                b = q * (piece // t) + i
+                q, copy = shift(lax.rem(3 * (j * PAIR + e), N_REP), i)
+                copies.append(copy)
+                b = q * strips + i
                 n = counts[b]
                 left = jnp.concatenate(
                     [jnp.where(k < n, blocks[b, k], jnp.zeros((), BF16)) for k in range(slots)],
                     axis=1,
                 )
                 right = jnp.concatenate([full[cols[k, b]] for k in range(slots)], axis=0)
-                dst[pl.ds(pl.multiple_of(i * t, t), t), :] = jnp.dot(
-                    left, right, preferred_element_type=F32
-                ).astype(BF16)
-
-    def shift(d):
-        q = here.peer_at(d)
-        return q, pltpu.make_async_remote_copy(
-            src_ref=mixed.at[q], dst_ref=m.at[here.rep],
-            send_sem=m_send.at[d - 1], recv_sem=m_recv.at[d - 1],
-            device_id=(here.row, q), device_id_type=MESH,
-        )
-
-    @pl.loop(1, N_REP)
-    def _(e):
-        q, copy = shift(lax.rem(3 * e, N_REP))
-        mix(mixed.at[q], q)
-        copy.start()
-
-    mix(m.at[here.rep], here.rep)
-    for d, q in enumerate(peers):
-        arrived(m.at[q], m_recv.at[d])
-
-    for i in range(piece // STRIP):
-        at = pl.ds(i * STRIP, STRIP)
+                mixed[q, at, :] = jnp.dot(left, right, preferred_element_type=F32).astype(BF16)
+
+            @pl.when(j > 0)
+            def _():
+                copies[0].start()
+
+            for copy in copies[1:]:
+                copy.start()
+
+        m[here.rep, at, :] = mixed[here.rep, at, :]
+
+    def whole(i):
+        at = pl.ds(i * t, t)
+        for d, q in enumerate(peers):
+            arrived(m.at[q, at], m_recv.at[d, i])
         x = jnp.concatenate([m[r, at, :] for r in range(N_REP)], axis=1)
         c = jnp.concatenate([cots[r, at, :] for r in range(N_REP)], axis=1)
         pre = jnp.dot(x, w[...], preferred_element_type=F32)
@@ -242,6 +246,12 @@
             back[r, at, :] = b[:, r * width : (r + 1) * width]
         for d, q in enumerate(peers):
             send(back.at[q, at], mixed_grad.at[here.rep, at], back_recv.at[d, i], (here.row, q))
+
+    mix(0)
+    for i in range(1, strips):
+        mix(i)
+        whole(i - 1)
+    whole(strips - 1)
     last = pltpu.make_async_copy(back.at[here.rep], mixed_grad.at[here.rep], local_sems.at[4])
     last.start()
     for r in range(N_REP):
@@ -250,10 +260,11 @@
         ).astype(BF16)
     last.wait()
     for d, q in enumerate(peers):
-        for i in range(piece // STRIP):
-            arrived(mixed_grad.at[q, pl.ds(i * STRIP, STRIP)], back_recv.at[d, i])
+        for i in range(strips):
+            arrived(mixed_grad.at[q, pl.ds(i * t, t)], back_recv.at[d, i])
     for d in range(1, N_REP):
-        shift(d)[1].wait_send()
+        for i in range(strips):
+            shift(d, i)[1].wait_send()
     send.finish()
 
 
@@ -261,7 +272,7 @@
     rows, width = features.shape
     n_blocks, _, t, _ = tiles.shape
     piece = rows // N_REP
-    strips = piece // STRIP
+    strips = piece // t
     dma = pltpu.SemaphoreType.DMA
     smem = pl.BlockSpec(memory_space=pltpu.SMEM)
     stack = pltpu.VMEM((N_REP, piece, width), BF16)
@@ -284,7 +295,8 @@
             pltpu.VMEM((piece, N_REP * width), BF16),
             stack,
             dma((15 * CHUNKS + 21 + 7 * strips,)), dma((15, CHUNKS)),
-            dma((7,)), dma((7,)), dma((7,)), dma((7,)), dma((7,)), dma((7, strips)), dma((5,)),
+            dma((7,)), dma((7,)), dma((7,)), dma((7, strips)), dma((7, strips)), dma((7, strips)),
+            dma((5,)),
         ],
         compiler_params=pltpu.CompilerParams(
             collective_id=0, has_side_effects=True, vmem_limit_bytes=60 * 1024 * 1024
@@ -350,7 +362,7 @@
         arrived(theirs.at[r, rows(i)], sib_recv.at[r, i])
         target = own.at[r] if dst is None else dst
 
-        @pl.loop(0, step // SUM_ROWS)
+        @pl.loop(0, step // SUM_ROWS, unroll=2)
         def _(j):
             at = pl.ds(pl.multiple_of(i * step + j * SUM_ROWS, SUM_ROWS), SUM_ROWS)
             acc = own[r, at, :].astype(F32) + theirs[r, at, :].astype(F32)

time: 216 us -> 212 us (0.981)
  Pallas kernels: 215 us -> 211 us
    pallas_call x1, Pallas kernels: 111 us -> 108 us  [forward(): pl.pallas_call(forward_kernel, in_specs=[ANY] * 4 + [smem] * 2, out_specs...]
where the time goes in v8:
time: 212 us
  Pallas kernels  211 us (100%)
    pallas_call x1, Pallas kernels, forward(): pl.pallas_call(forward_kernel, in_specs=[ANY] * 4 + [smem] * 2, out_specs...  108 us
    pallas_call x1, Pallas kernels, reduce_all(): pl.pallas_call(reduce_kernel, in_specs=[ANY] * 3, out_specs=[ANY, VM, VM]...  77.5 us
    pallas_call x1, Pallas kernels, spmm_t(): pl.pallas_call(bwd_kernel, grid_spec=pltpu.PrefetchScalarGridSpec(num_sca...  21.6 us

profile of v8, /device:TPU:1, one launch (start us, length us, event | category | flops | bytes accessed | tf_op | source)
XLA Modules:
  0.0 211.8 jit_solution(600937715511716533)
XLA Ops:
  0.6 108.2 %forward.1 = (bf16[8,512,128]{2,1,0:T(8,128)(2,1)}, bf16[8,512,128]{2,1,0:T(8,128)(2,1)}, bf16[8,128,1024]{2,1,0:T(8,128)(2,1)}) custom-call(bf16[32,128,128]{2,1,0:T(8,128)(2,1)} %bitcast.7, bf16[4096,128]{1,0:T(8,128)(2,1)} %cot.1, bf16[1024,128]{1,0:T(8,128)(2,1)} %weight.1, bf16[32,16,128,128]{3,2,1,0:T(8,128)(2,1)} %tiles.3, s32[16,32]{1,0:T(8,128)} %bitcast.10, ...), custom_call_target="tpu_custom_call" | custom-call | tf_op jit(solution)/shard_map/forward/pallas_call | solution.py:279
  108.9 21.6 %spmm_t.1 = bf16[512,128,128]{2,1,0:T(8,128)(2,1)} custom-call(s32[16,32]{1,0:T(8,128)} %bitcast.11, s32[32]{0:T(128)} %counts.3, bf16[32,16,128,128]{3,2,1,0:T(8,128)(2,1)} %tiles.3, bf16[4096,128]{1,0:T(8,128)(2,1)} %bitcast.9), custom_call_target="tpu_custom_call" | custom-call | tf_op jit(solution)/shard_map/spmm_t/pallas_call | solution.py:629
  130.5 77.5 %reduce_all.1 = (bf16[8,512,128]{2,1,0:T(8,128)(2,1)}, bf16[4096,128]{1,0:T(8,128)(2,1)}, f32[128,64]{1,0:T(8,128)}) custom-call(bf16[16,4096,128]{2,1,0:T(8,128)(2,1)} %bitcast.6, bf16[8,512,128]{2,1,0:T(8,128)(2,1)} %get-tuple-element.13.act, bf16[8,128,1024]{2,1,0:T(8,128)(2,1)} %get-tuple-element.14.wgrad), custom_call_target="tpu_custom_call" | custom-call | tf_op jit(solution)/shard_map/reduce_all/pallas_call | solution.py:506
  208.0 3.8 %settle.1 = (bf16[4096,128]{1,0:T(8,128)(2,1)}, bf16[4096,128]{1,0:T(8,128)(2,1)}, f32[64,128]{1,0:T(8,128)}) custom-call(bf16[4096,128]{1,0:T(8,128)(2,1)} %bitcast.8, bf16[4096,128]{1,0:T(8,128)(2,1)} %get-tuple-element.16.b, f32[128,64]{1,0:T(8,128)} %get-tuple-element.17.w), custom_call_target="tpu_custom_call" | custom-call | tf_op jit(solution)/shard_map/settle/pallas_call | solution.py:676

commit v9 on v8

--- a/solution.py
+++ b/solution.py
@@ -133,6 +133,11 @@
     slots_of = [here.slot(*column) for column in columns]
     opposite = [(i + CHUNKS // 2) % CHUNKS for i in range(CHUNKS)]
 
+    mine = pl.ds(pl.multiple_of(here.c * half, half), half)
+    theirs = pl.ds(pl.multiple_of((1 - here.c) * half, half), half)
+    beside = peers[3]
+    for d in (4, 1, 2, 3):
+        send(weight.at[mine], ws.at[here.rep, mine], w_recv.at[d - 1], (here.row, peers[d - 1]))
     for i in range(CHUNKS):
         send(feats.at[rows(i)], place(here.row, i), recv_sems.at[3, i], across)
     for a, b in enumerate(opposite):
@@ -140,10 +145,6 @@
         send(feats.at[rows(b)], place(here.row, b), recv_sems.at[1, b], down)
     for i in range(CHUNKS):
         send(feats.at[rows(i)], place(here.row, i), recv_sems.at[7, i], sib)
-    mine = pl.ds(pl.multiple_of(here.c * half, half), half)
-    theirs = pl.ds(pl.multiple_of((1 - here.c) * half, half), half)
-    for d, q in enumerate(peers):
-        send(weight.at[mine], ws.at[here.rep, mine], w_recv.at[d], (here.row, q))
     for d, q in enumerate(peers):
         send(
             cot.at[pl.ds(pl.multiple_of(q * piece, piece), piece)],
@@ -172,12 +173,19 @@
                     send(src, src, recv_sems.at[4, a], up)
                     send(src, src, recv_sems.at[5, a], down)
                 send(src, src, recv_sems.at[11, a], sib)
+        if k == 0:
+            arrived(ws.at[beside, mine], w_recv.at[3])
+            for d in (1, 2, 3):
+                send(
+                    ws.at[beside, mine], ws.at[beside, mine], w_recv.at[d + 3],
+                    (here.row, peers[d - 1]),
+                )
         for i in range(CHUNKS):
             take(k + 2, i)
-        if k == 0:
-            for d, q in enumerate(peers):
-                arrived(ws.at[q, mine], w_recv.at[d])
-                send(ws.at[q, mine], ws.at[q, mine], w_sib.at[d], sib)
+    for d, q in enumerate(peers):
+        if d != 3:
+            arrived(ws.at[q, mine], w_recv.at[d])
+        send(ws.at[q, mine], ws.at[q, mine], w_sib.at[d], sib)
 
     for d, q in enumerate(peers):
         arrived(ws.at[q, theirs], w_sib.at[d])
@@ -312,7 +320,7 @@
 def reduce_kernel(
     part, act, wgrad, act_out, out, wg_out,
     own, theirs, far_up, far_down, near_up, near_down, cross, early, own_act,
-    wg_own, wg_sib, wg_in, wg_half, wg_row, wg_fin, wg_fin_sib,
+    wg_own, wg_sib, wg_in, wg_x, wg_half, wg_row, wg_fin, wg_fin_sib,
     send_sems, load_sems, sib_recv, far_recv, near_recv, cross_recv, early_recv,
     act_recv, wg_recv, row_recv, pair_recv, local_sems,
 ):
@@ -444,24 +452,39 @@
     def _(j):
         wg_own[j] = (wg_own[j].astype(F32) + wg_sib[j].astype(F32)).astype(BF16)
 
-    for d, q in enumerate(peers):
-        send(wg_own.at[q], wg_in.at[d], wg_recv.at[d], (here.row, q))
+    for d in range(3):
+        to = (here.row, peers[d])
+        send(wg_own.at[peers[d + 4]], wg_in.at[d], wg_recv.at[d], to)
+        send(wg_own.at[peers[d]], wg_in.at[d + 3], wg_recv.at[d + 3], to)
     for d, q in enumerate(peers):
         send(act.at[q], act_out.at[here.rep], act_recv.at[d], (here.row, q))
     extra[0].wait()
     keep = pltpu.make_async_copy(own_act, act_out.at[here.rep], local_sems.at[0])
     keep.start()
     far(1)
+
+    for d in range(3):
+        arrived(wg_in.at[d], wg_recv.at[d])
+
+    @pl.loop(0, wg_half.shape[0])
+    def _(j):
+        at = pl.ds(pl.multiple_of(j * 128, 128), 128)
+        acc = wg_own[peers[3], :, at].astype(F32)
+        for d in range(3):
+            acc = acc + wg_in[d, :, at].astype(F32)
+        wg_x[:, at] = acc.astype(BF16)
+
+    send(wg_x, wg_in.at[6], wg_recv.at[6], (here.row, peers[3]))
     near_last(0)
 
-    for d in range(N_REP - 1):
+    for d in range(3, 7):
         arrived(wg_in.at[d], wg_recv.at[d])
 
     @pl.loop(0, wg_half.shape[0])
     def _(j):
         at = pl.ds(pl.multiple_of(j * 128, 128), 128)
         acc = wg_own[here.rep, :, at].astype(F32)
-        for d in range(N_REP - 1):
+        for d in range(3, 7):
             acc = acc + wg_in[d, :, at].astype(F32)
         wg_half[j] = acc.astype(BF16)
 
@@ -525,6 +548,7 @@
             pltpu.VMEM((n_rep, edge, wide), BF16),
             pltpu.VMEM((n_rep, edge, wide), BF16),
             pltpu.VMEM((n_rep - 1, edge, wide), BF16),
+            pltpu.VMEM((edge, wide), BF16),
             pltpu.VMEM((wide // 128, edge, 128), BF16),
             pltpu.VMEM((7, edge, 128), BF16),
             pltpu.VMEM((edge, 128), F32),

time: 212 us -> 210 us (level)
  no operation moved by 1% of the time
where the time goes in v9:
time: 210 us
  Pallas kernels  209 us (100%)
    pallas_call x1, Pallas kernels, forward(): pl.pallas_call(forward_kernel, in_specs=[ANY] * 4 + [smem] * 2, out_specs...  107 us
    pallas_call x1, Pallas kernels, reduce_all(): pl.pallas_call(reduce_kernel, in_specs=[ANY] * 3, out_specs=[ANY, VM, VM]...  75.7 us
    pallas_call x1, Pallas kernels, spmm_t(): pl.pallas_call(bwd_kernel, grid_spec=pltpu.PrefetchScalarGridSpec(num_sca...  22.6 us

profile of v9, /device:TPU:1, one launch (start us, length us, event | category | flops | bytes accessed | tf_op | source)
XLA Modules:
  0.0 209.7 jit_solution(5742357477142850342)
XLA Ops:
  0.6 107.0 %forward.1 = (bf16[8,512,128]{2,1,0:T(8,128)(2,1)}, bf16[8,512,128]{2,1,0:T(8,128)(2,1)}, bf16[8,128,1024]{2,1,0:T(8,128)(2,1)}) custom-call(bf16[32,128,128]{2,1,0:T(8,128)(2,1)} %bitcast.7, bf16[4096,128]{1,0:T(8,128)(2,1)} %cot.1, bf16[1024,128]{1,0:T(8,128)(2,1)} %weight.1, bf16[32,16,128,128]{3,2,1,0:T(8,128)(2,1)} %tiles.3, s32[16,32]{1,0:T(8,128)} %bitcast.10, ...), custom_call_target="tpu_custom_call" | custom-call | tf_op jit(solution)/shard_map/forward/pallas_call | solution.py:287
  107.6 22.6 %spmm_t.1 = bf16[512,128,128]{2,1,0:T(8,128)(2,1)} custom-call(s32[16,32]{1,0:T(8,128)} %bitcast.11, s32[32]{0:T(128)} %counts.3, bf16[32,16,128,128]{3,2,1,0:T(8,128)(2,1)} %tiles.3, bf16[4096,128]{1,0:T(8,128)(2,1)} %bitcast.9), custom_call_target="tpu_custom_call" | custom-call | tf_op jit(solution)/shard_map/spmm_t/pallas_call | solution.py:653
  130.2 75.7 %reduce_all.1 = (bf16[8,512,128]{2,1,0:T(8,128)(2,1)}, bf16[4096,128]{1,0:T(8,128)(2,1)}, f32[128,64]{1,0:T(8,128)}) custom-call(bf16[16,4096,128]{2,1,0:T(8,128)(2,1)} %bitcast.6, bf16[8,512,128]{2,1,0:T(8,128)(2,1)} %get-tuple-element.13.act, bf16[8,128,1024]{2,1,0:T(8,128)(2,1)} %get-tuple-element.14.wgrad), custom_call_target="tpu_custom_call" | custom-call | tf_op jit(solution)/shard_map/reduce_all/pallas_call | solution.py:529
  205.9 3.8 %settle.1 = (bf16[4096,128]{1,0:T(8,128)(2,1)}, bf16[4096,128]{1,0:T(8,128)(2,1)}, f32[64,128]{1,0:T(8,128)}) custom-call(bf16[4096,128]{1,0:T(8,128)(2,1)} %bitcast.8, bf16[4096,128]{1,0:T(8,128)(2,1)} %get-tuple-element.16.b, f32[128,64]{1,0:T(8,128)} %get-tuple-element.17.w), custom_call_target="tpu_custom_call" | custom-call | tf_op jit(solution)/shard_map/settle/pallas_call | solution.py:700

commit v10 on v9

--- a/solution.py
+++ b/solution.py
@@ -145,11 +145,6 @@
         send(feats.at[rows(b)], place(here.row, b), recv_sems.at[1, b], down)
     for i in range(CHUNKS):
         send(feats.at[rows(i)], place(here.row, i), recv_sems.at[7, i], sib)
-    for d, q in enumerate(peers):
-        send(
-            cot.at[pl.ds(pl.multiple_of(q * piece, piece), piece)],
-            cots.at[here.rep], cot_recv.at[d], (here.row, q),
-        )
     for copy in own:
         copy.start()
 
@@ -182,6 +177,12 @@
                 )
         for i in range(CHUNKS):
             take(k + 2, i)
+        if k == 0:
+            for d, q in enumerate(peers):
+                send(
+                    cot.at[pl.ds(pl.multiple_of(q * piece, piece), piece)],
+                    cots.at[here.rep], cot_recv.at[d], (here.row, q),
+                )
     for d, q in enumerate(peers):
         if d != 3:
             arrived(ws.at[q, mine], w_recv.at[d])
@@ -370,7 +371,7 @@
         arrived(theirs.at[r, rows(i)], sib_recv.at[r, i])
         target = own.at[r] if dst is None else dst
 
-        @pl.loop(0, step // SUM_ROWS, unroll=2)
+        @pl.loop(0, step // SUM_ROWS, unroll=4)
         def _(j):
             at = pl.ds(pl.multiple_of(i * step + j * SUM_ROWS, SUM_ROWS), SUM_ROWS)
             acc = own[r, at, :].astype(F32) + theirs[r, at, :].astype(F32)

time: 210 us -> 209 us (level)
  no operation moved by 1% of the time
where the time goes in v10:
time: 209 us
  Pallas kernels  208 us (100%)
    pallas_call x1, Pallas kernels, forward(): pl.pallas_call(forward_kernel, in_specs=[ANY] * 4 + [smem] * 2, out_specs...  107 us
    pallas_call x1, Pallas kernels, reduce_all(): pl.pallas_call(reduce_kernel, in_specs=[ANY] * 3, out_specs=[ANY, VM, VM]...  75.3 us
    pallas_call x1, Pallas kernels, spmm_t(): pl.pallas_call(bwd_kernel, grid_spec=pltpu.PrefetchScalarGridSpec(num_sca...  22 us

profile of v10, /device:TPU:1, one launch (start us, length us, event | category | flops | bytes accessed | tf_op | source)
XLA Modules:
  0.0 208.8 jit_solution(17026730042995809877)
XLA Ops:
  0.6 107.0 %forward.1 = (bf16[8,512,128]{2,1,0:T(8,128)(2,1)}, bf16[8,512,128]{2,1,0:T(8,128)(2,1)}, bf16[8,128,1024]{2,1,0:T(8,128)(2,1)}) custom-call(bf16[32,128,128]{2,1,0:T(8,128)(2,1)} %bitcast.7, bf16[4096,128]{1,0:T(8,128)(2,1)} %cot.1, bf16[1024,128]{1,0:T(8,128)(2,1)} %weight.1, bf16[32,16,128,128]{3,2,1,0:T(8,128)(2,1)} %tiles.3, s32[16,32]{1,0:T(8,128)} %bitcast.10, ...), custom_call_target="tpu_custom_call" | custom-call | tf_op jit(solution)/shard_map/forward/pallas_call | solution.py:288
  107.6 22.0 %spmm_t.1 = bf16[512,128,128]{2,1,0:T(8,128)(2,1)} custom-call(s32[16,32]{1,0:T(8,128)} %bitcast.11, s32[32]{0:T(128)} %counts.3, bf16[32,16,128,128]{3,2,1,0:T(8,128)(2,1)} %tiles.3, bf16[4096,128]{1,0:T(8,128)(2,1)} %bitcast.9), custom_call_target="tpu_custom_call" | custom-call | tf_op jit(solution)/shard_map/spmm_t/pallas_call | solution.py:654
  129.6 75.3 %reduce_all.1 = (bf16[8,512,128]{2,1,0:T(8,128)(2,1)}, bf16[4096,128]{1,0:T(8,128)(2,1)}, f32[128,64]{1,0:T(8,128)}) custom-call(bf16[16,4096,128]{2,1,0:T(8,128)(2,1)} %bitcast.6, bf16[8,512,128]{2,1,0:T(8,128)(2,1)} %get-tuple-element.13.act, bf16[8,128,1024]{2,1,0:T(8,128)(2,1)} %get-tuple-element.14.wgrad), custom_call_target="tpu_custom_call" | custom-call | tf_op jit(solution)/shard_map/reduce_all/pallas_call | solution.py:530
  204.9 3.8 %settle.1 = (bf16[4096,128]{1,0:T(8,128)(2,1)}, bf16[4096,128]{1,0:T(8,128)(2,1)}, f32[64,128]{1,0:T(8,128)}) custom-call(bf16[4096,128]{1,0:T(8,128)(2,1)} %bitcast.8, bf16[4096,128]{1,0:T(8,128)(2,1)} %get-tuple-element.16.b, f32[128,64]{1,0:T(8,128)} %get-tuple-element.17.w), custom_call_target="tpu_custom_call" | custom-call | tf_op jit(solution)/shard_map/settle/pallas_call | solution.py:701
